TPU v7x, 32 devices: a whole 2x2x4 slice. The times are simulated.
32 devices in a mesh: grp: 4 (over x, core), tp: 4 (over z), cores: 2 (over y).
Axes of the slice: x: 2, y: 2, z: 4, core: 2. Of those that a mesh axis runs over, the one named last changes fastest.
Arguments:
- tokens: bfloat16 [4096, 8192], P('grp', ('tp', 'cores')), may hold values from -6 to 6
- gate_up_weight: bfloat16 [8192, 2, 16384], P(None, None, ('tp', 'cores')), may hold values from -0.0625 to 0.0625
- down_factor_pool: bfloat16 [8, 8192, 256], P(('tp', 'cores'), 'grp'), may hold values from -0.0625 to 0.0625
- up_factor_pool: bfloat16 [8, 4, 8, 128, 1024], P(('tp', 'cores'), 'grp'), may hold values from -0.5 to 0.5
- segment_adapters: int32 [4, 3], replicated, may hold values from 0 to 7
- segment_tile_counts: int32 [4, 3], P('grp'), may hold values from 1 to 4, 8 in all within a row
- adapter_pool_rows: int32 [8], replicated, may hold values from 0 to 7, each once
Outputs:
- hidden: bfloat16 [4096, 16384], P('grp', ('tp', 'cores'))
Inputs may be any that keep to these rules, and one draw needn't show every extreme that they name: `segment_tile_counts`: each row sums to 8. `adapter_pool_rows`: each pool row appears once.
All inputs are finite; a program needn't handle non-finite values.
Results may differ from a plain program's by a relative error of at most 0.0036.
Values may be sent and summed in bfloat16 or wider, within the bound.
A program may use at most 320 MiB of HBM per device.

v0:
```python
import jax
import jax.numpy as jnp
from jax import lax
from jax.sharding import PartitionSpec as P

TILE = 128


adapter_scale = 0.5


def tile_segments(tile_lengths, tile_count):
    bounds = jnp.cumsum(tile_lengths)
    positions = jnp.arange(tile_count, dtype=jnp.int32)
    return jnp.sum((bounds[None, :] <= positions[:, None]).astype(jnp.int32), axis=1)


def per_device(
    tokens,
    gate_up_weight,
    down_factor_pool,
    up_factor_pool,
    segment_adapters,
    segment_tile_counts,
    adapter_pool_rows,
):
    groups = lax.axis_size("grp")
    device_shares = lax.axis_size(("tp", "cores"))
    piece_index = lax.axis_index(("tp", "cores"))
    token_count = tokens.shape[0]
    full_width = tokens.shape[1] * device_shares
    local_hidden_width = gate_up_weight.shape[2]
    twice_rank = down_factor_pool.shape[2]
    rank_size = twice_rank // 2
    share_rows = down_factor_pool.shape[1] // device_shares
    local_count = down_factor_pool.shape[0]
    seg_count = segment_adapters.shape[1]
    narrow = local_hidden_width // groups
    local_down_factor = down_factor_pool.reshape(
        local_count, device_shares, share_rows * twice_rank
    )
    local_up_factor = up_factor_pool.reshape(local_count, device_shares, -1)
    a_spread, b_spread = (
        lax.all_to_all(local_down_factor, ("tp", "cores"), split_axis=1, concat_axis=0, tiled=True),
        lax.all_to_all(local_up_factor, ("tp", "cores"), split_axis=1, concat_axis=0, tiled=True),
    )
    all_slots = jnp.take(adapter_pool_rows, segment_adapters)
    a_wanted = jnp.take(a_spread, all_slots, axis=0)
    b_wanted = jnp.take(b_spread, all_slots, axis=0)
    a_arrived, b_arrived = (
        lax.all_to_all(a_wanted, "grp", split_axis=0, concat_axis=2, tiled=True),
        lax.all_to_all(b_wanted, "grp", split_axis=0, concat_axis=2, tiled=True),
    )
    a_chosen = a_arrived.reshape(seg_count, groups, -1)
    b_chosen = b_arrived.reshape(seg_count, groups, -1)
    gathered = lax.all_gather(tokens, ("tp", "cores"), axis=1, tiled=True)
    frozen_output = jnp.dot(
        gathered,
        gate_up_weight.reshape(full_width, 2 * local_hidden_width),
        preferred_element_type=jnp.float32,
    )
    frozen_output = frozen_output.reshape(token_count, 2, local_hidden_width)
    tile_count = token_count // TILE
    tile_seg = tile_segments(segment_tile_counts[0], tile_count)
    a_tiles = jnp.take(a_chosen, tile_seg, axis=0).reshape(
        tile_count, groups * share_rows, twice_rank
    )
    own_features = lax.dynamic_slice_in_dim(
        gathered.reshape(token_count, groups, device_shares, share_rows), piece_index, 1, axis=2
    )
    own_features = own_features.reshape(tile_count, TILE, groups * share_rows)
    partial_shrink = jnp.einsum(
        "tkd,tdr->tkr", own_features, a_tiles, preferred_element_type=jnp.float32
    )
    reduced_input = lax.psum(partial_shrink, ("tp", "cores")).astype(jnp.bfloat16)
    b_tiles = jnp.take(b_chosen, tile_seg, axis=0).reshape(tile_count, groups, rank_size, 2, narrow)
    gate_adapter_delta = jnp.einsum(
        "tkr,tmrw->tkmw",
        reduced_input[:, :, :rank_size],
        b_tiles[:, :, :, 0, :],
        preferred_element_type=jnp.float32,
    )
    up_adapter_delta = jnp.einsum(
        "tkr,tmrw->tkmw",
        reduced_input[:, :, rank_size:],
        b_tiles[:, :, :, 1, :],
        preferred_element_type=jnp.float32,
    )
    gate_combined = frozen_output[:, 0, :] + adapter_scale * gate_adapter_delta.reshape(
        token_count, local_hidden_width
    )
    up_combined = frozen_output[:, 1, :] + adapter_scale * up_adapter_delta.reshape(
        token_count, local_hidden_width
    )
    return (jax.nn.silu(gate_combined) * up_combined).astype(jnp.bfloat16)


def solution(mesh):
    return jax.shard_map(
        per_device,
        mesh=mesh,
        in_specs=(
            P("grp", ("tp", "cores")),
            P(None, None, ("tp", "cores")),
            P(("tp", "cores"), "grp", None),
            P(("tp", "cores"), "grp", None, None, None),
            P(),
            P("grp", None),
            P(),
        ),
        out_specs=P("grp", ("tp", "cores")),
        check_vma=False,
    )
```

profile of v0, /device:TPU:0, one launch (start us, length us, event | category | flops | bytes accessed | tf_op | source)
XLA Modules:
  0.0 634.6 jit_solution(12954752661760870075)
XLA Ops:
  11.1 7.3 %reduce.3 = bf16[8,65536]{1,0:T(8,128)(2,1)S(1)} reduce(bf16[8,1,65536]{2,1,0:T(2,128)(2,1)S(1)} %bitcast.106, bf16[]{:T(256)} %broadcast.154), dimensions={1}, to_apply=%bitcast.85.reduce_sub_computation | reduce | bytes 2097154
  20.3 7.6 %all-to-all-start = ((bf16[8,2,32768]{2,1,0:T(2,128)(2,1)}), bf16[8,2,32768]{2,1,0:T(2,128)(2,1)S(1)}, u32[]{:S(2)}, u32[]{:S(2)}) async-start(bf16[8,2,32768]{2,1,0:T(2,128)(2,1)} %reshape.206), calls=%async_computation | async-start | bytes 2097152 | tf_op jit(solution)/shard_map/all_to_all | solution.py:44
  33.0 13.0 %reduce.2 = bf16[8,131072]{1,0:T(8,128)(2,1)S(1)} reduce(bf16[8,1,131072]{2,1,0:T(2,128)(2,1)} %bitcast.100, bf16[]{:T(256)} %broadcast.154), dimensions={1}, to_apply=%bitcast.83.reduce_sub_computation | reduce | bytes 4194306
  49.2 4.4 all-to-all-done
  58.2 5.8 reshape.207
  77.8 28.9 %all-to-all-done.2 = bf16[8,2,65536]{2,1,0:T(2,128)(2,1)S(1)} async-done(((bf16[8,2,65536]{2,1,0:T(2,128)(2,1)}), bf16[8,2,65536]{2,1,0:T(2,128)(2,1)S(1)}, u32[]{:S(2)}, u32[]{:S(2)}) %all-to-all-start.2) | async-done | bytes 2097184 | tf_op jit(solution)/shard_map/all_to_all | solution.py:45
  106.7 5.0 all-to-all-start.1
  116.0 4.5 copy.79
  132.0 5.8 fusion.8
  137.8 5.0 all-to-all-start.3
  143.7 45.1 %copy.69 = bf16[1024,8,2,2048]{3,1,2,0:T(8,128)(2,1)} copy(bf16[1024,8,2,2048]{3,2,1,0:T(2,128)(2,1)} %bitcast.33) | data formatting | bytes 134217728
  188.8 83.4 %copy.48 = bf16[4096,8192]{1,0:T(8,128)(2,1)} copy(bf16[4096,8192]{0,1:T(8,128)(2,1)} %bitcast.1) | data formatting | bytes 134217728 | tf_op jit(solution)/shard_map/dot_general | solution.py:57
  275.4 5.4 gather_fusion.2
  280.8 7.9 %gather.27 = bf16[8,1024,256]{2,1,0:T(8,128)(2,1)} reshape(bf16[8,4,65536]{2,1,0:T(4,128)(2,1)} %gather_fusion.2) | data formatting | bytes 8388608 | tf_op jit(solution)/shard_map/jit(_take)/gather | solution.py:65
  288.7 5.2 copy.78
  295.0 5.4 gather_fusion.5
  300.4 5.6 gather_fusion.6
  305.9 8.3 %pad_maximum_fusion = bf16[8,4,131072]{2,1,0:T(4,128)(2,1)} fusion(bf16[8,4,65536]{2,1,0:T(4,128)(2,1)} %gather_fusion.6, bf16[8,4,65536]{2,1,0:T(4,128)(2,1)} %gather_fusion.5), kind=kLoop, calls=%fused_computation.15 | loop fusion | flops 16777216 | bytes 16777216
  314.3 12.5 %reshape.201 = bf16[8,4,128,2,512]{4,3,2,1,0:T(2,128)(2,1)} reshape(bf16[8,4,131072]{2,1,0:T(4,128)(2,1)} %pad_maximum_fusion) | data formatting | bytes 16777216 | tf_op jit(solution)/shard_map/jit(_take)/gather | solution.py:76
  326.8 8.2 %copy_select_fusion = bf16[8,4,128,2,512]{4,2,1,0,3:T(8,128)(2,1)} fusion(bf16[8,4,128,2,512]{4,3,2,1,0:T(2,128)(2,1)} %reshape.201, pred[8]{0:T(512)(128)(4,1)S(1)} %compare_and_fusion.1), kind=kLoop, calls=%fused_computation.16 | loop fusion | flops 4194304 | bytes 16777224 | tf_op jit(solution)/shard_map/jit(_take)/select_n | solution.py:76
  335.0 37.6 %all-gather.2.cloned.1.call-done = bf16[1024,8192]{1,0:T(8,128)(2,1)} async-done(((bf16[1024,1024]{1,0:T(8,128)(2,1)}), bf16[1024,8192]{1,0:T(8,128)(2,1)}) %all-gather.2.cloned.1.call-update) | async-done | bytes 16777232 | tf_op jit(solution)/shard_map/all_gather | solution.py:56
  372.6 10.3 %copy.70 = bf16[128,8,32,256]{3,2,1,0:T(8,128)(2,1)S(1)} copy(bf16[128,8,32,256]{3,1,2,0:T(8,128)(2,1)} %bitcast.102) | data formatting | bytes 33554432
  382.9 13.7 %dynamic-slice_reduce_fusion = bf16[1024,4,256]{2,1,0:T(4,128)(2,1)S(1)} fusion(bf16[1024,4,8,256]{3,2,1,0:T(8,128)(2,1)S(1)} %bitcast.98, s32[]{:T(128)S(6)} %select_n.80), kind=kLoop, calls=%fused_computation.27 | loop fusion | bytes 4194308 | tf_op jit(solution)/shard_map/dynamic_slice | solution.py:68
  403.1 70.2 %all-reduce.1 = bf16[8,128,256]{2,1,0:T(8,128)(2,1)S(1)} all-reduce(f32[8,128,256]{2,1,0:T(8,128)S(1)} %fusion.9), channel_id=1, replica_groups=mesh['grp'=4,'tp'=4,'cores'=2] {'tp','cores'}, use_global_device_ids=true, to_apply=%region_2.3 | all-reduce | flops 262144 | bytes 1572864 | tf_op jit(solution)/shard_map/psum | solution.py:75
  473.2 6.6 %broadcast_multiply_fusion.1 = f32[8,128,4,512]{3,1,2,0:T(8,128)} fusion(bf16[8,4,128,2,512]{4,2,1,0,3:T(8,128)(2,1)} %copy_select_fusion, bf16[8,128,256]{2,1,0:T(8,128)(2,1)S(1)} %all-reduce.1), kind=kOutput, calls=%fused_computation.24 | convolution fusion | flops 538968064 | bytes 12845056 | tf_op jit(solution)/shard_map/tkr,tmrw->tkmw/dot_general | solution.py:77
  479.8 6.6 %broadcast_multiply_fusion = f32[8,128,4,512]{3,1,2,0:T(8,128)} fusion(bf16[8,4,128,2,512]{4,2,1,0,3:T(8,128)(2,1)} %copy_select_fusion, bf16[8,128,256]{2,1,0:T(8,128)(2,1)S(1)} %all-reduce.1), kind=kOutput, calls=%fused_computation.23 | convolution fusion | flops 538968064 | bytes 12845056 | tf_op jit(solution)/shard_map/tkr,tmrw->tkmw/dot_general | solution.py:83
  486.5 12.1 %copy.60 = f32[8,128,4,512]{3,2,1,0:T(4,128)} copy(f32[8,128,4,512]{3,1,2,0:T(8,128)} %broadcast_multiply_fusion) | data formatting | bytes 16777216 | tf_op jit(solution)/shard_map/mul | solution.py:92
  498.5 10.8 %copy.72 = f32[128,8,4,512]{3,1,2,0:T(8,128)} copy(f32[128,8,4,512]{3,2,1,0:T(4,128)} %bitcast.94) | data formatting | bytes 16777216
  509.4 12.1 %copy.59 = f32[8,128,4,512]{3,2,1,0:T(4,128)} copy(f32[8,128,4,512]{3,1,2,0:T(8,128)} %broadcast_multiply_fusion.1) | data formatting | bytes 16777216 | tf_op jit(solution)/shard_map/mul | solution.py:89
  521.5 10.8 %copy.71 = f32[128,8,4,512]{3,1,2,0:T(8,128)} copy(f32[128,8,4,512]{3,2,1,0:T(4,128)} %bitcast.95) | data formatting | bytes 16777216
  532.2 80.5 %fusion = f32[1024,2,2048]{2,0,1:T(8,128)} fusion(bf16[2,2048,8192]{2,1,0:T(8,128)(2,1)} %bitcast.2, bf16[1024,8192]{1,0:T(8,128)(2,1)} %all-gather.2.cloned.1.call-done), kind=kOutput, calls=%fused_computation.7 | convolution fusion | flops 68719476736 | bytes 100663296 | tf_op jit(solution)/shard_map/dot_general | solution.py:57
  612.8 14.8 %fusion.4 = bf16[1024,2048]{1,0:T(8,128)(2,1)} fusion(f32[1024,2048]{1,0:T(8,128)} %bitcast.96, f32[1024,2,2048]{2,0,1:T(8,128)} %fusion, f32[1024,2048]{1,0:T(8,128)} %bitcast.97), kind=kLoop, calls=%fused_computation.12 | loop fusion | flops 16777216 | bytes 37748736 | tf_op jit(solution)/shard_map/convert_element_type | solution.py:95
  (49 shorter events, 60.6 us)
Async XLA Ops:
  6.5 21.5 %copy-start = (s32[8]{0:T(128)S(1)}, s32[8]{0:T(128)}, u32[]{:S(2)}) copy-start(s32[8]{0:T(128)} %param.13) | copy-start | bytes 100
  10.5 17.4 %copy-start.4 = (s32[4,3]{1,0:T(4,128)S(1)}, s32[4,3]{1,0:T(4,128)}, u32[]{:S(2)}) copy-start(s32[4,3]{1,0:T(4,128)} %param.11) | copy-start | bytes 148
  18.4 10.5 %copy-start.3 = (bf16[1,1,8,128,1024]{4,3,2,1,0:T(8,128)(2,1)S(1)}, bf16[1,1,8,128,1024]{4,3,2,1,0:T(8,128)(2,1)}, u32[]{:S(2)}) copy-start(bf16[1,1,8,128,1024]{4,3,2,1,0:T(8,128)(2,1)} %param.10) | copy-start | bytes 6291460
  20.3 33.4 %all-to-all-start = ((bf16[8,2,32768]{2,1,0:T(2,128)(2,1)}), bf16[8,2,32768]{2,1,0:T(2,128)(2,1)S(1)}, u32[]{:S(2)}, u32[]{:S(2)}) async-start(bf16[8,2,32768]{2,1,0:T(2,128)(2,1)} %reshape.206), calls=%async_computation | async-start | bytes 2097152 | tf_op jit(solution)/shard_map/all_to_all | solution.py:44
  53.6 1.0 copy-start.2
  54.6 52.0 %all-to-all-start.2 = ((bf16[8,2,65536]{2,1,0:T(2,128)(2,1)}), bf16[8,2,65536]{2,1,0:T(2,128)(2,1)S(1)}, u32[]{:S(2)}, u32[]{:S(2)}) async-start(bf16[8,2,65536]{2,1,0:T(2,128)(2,1)} %reshape.204), calls=%async_computation.2 | async-start | bytes 4194304 | tf_op jit(solution)/shard_map/all_to_all | solution.py:45
  106.7 31.1 %all-to-all-start.1 = ((bf16[4,3,1,65536]{3,1,2,0:T(4,128)(2,1)}), bf16[4,3,1,65536]{3,1,2,0:T(4,128)(2,1)}, u32[]{:S(2)}, u32[]{:S(2)}) async-start(bf16[4,3,1,65536]{3,1,2,0:T(4,128)(2,1)} %select_bitcast_fusion), calls=%async_computation.1 | async-start | bytes 4194304 | tf_op jit(solution)/shard_map/all_to_all | solution.py:51
  137.8 5.7 copy-start.5
  137.8 150.9 %all-to-all-start.3 = ((bf16[4,3,1,131072]{3,1,2,0:T(4,128)(2,1)}), bf16[4,3,1,131072]{3,1,2,0:T(4,128)(2,1)}, u32[]{:S(2)}, u32[]{:S(2)}) async-start(bf16[4,3,1,131072]{3,1,2,0:T(4,128)(2,1)} %fusion.8), calls=%async_computation.3 | async-start | bytes 8388608 | tf_op jit(solution)/shard_map/all_to_all | solution.py:52
  142.8 229.8 %all-gather.2.cloned.1.call-start = ((), (), s32[]{:S(2)}) async-start(), calls=%async_computation.4 | async-start | bytes 18874368 | tf_op jit(solution)/shard_map/all_gather | solution.py:56
  612.8 14.8 %copy-start.1 = (s32[8]{0:T(128)S(1)}, s32[8]{0:T(128)}, u32[]{:S(2)}) copy-start(s32[8]{0:T(128)} %param.13) | copy-start | bytes 100
Sparse Core Ops, SparseCore 0:
  145.8 226.8 all-gather.1
where the time goes:
time: 644 us; the launch traced here: 635 us
  local copies, waits for them, and re-layouts  299 us (46%)
  matrix products  97.6 us (15%)
  waiting for transfers between devices  71.4 us (11%)
  blocking collectives  70.2 us (11%)
  other arithmetic  61.6 us (10%)
  starting transfers between devices  21.4 us (3%)
  between operations  13.8 us (2%)
    unnamed x23, local copies, waits for them, and re-layouts  101 us
    dot_general x1, local copies, waits for them, and re-layouts, per_device(): jnp.dot(gathered, gate_up_weight.reshape(full_width, 2 * local_hidden_wid...  83.4 us
    dot_general x1, matrix products, per_device(): jnp.dot(gathered, gate_up_weight.reshape(full_width, 2 * local_hidden_wid...  80.5 us
    psum x1, blocking collectives, per_device(): lax.psum(partial_shrink, ('tp', 'cores')).astype(jnp.bfloat16)  70.2 us
    all_gather x1, waiting for transfers between devices, per_device(): gathered = lax.all_gather(tokens, ('tp', 'cores'), axis=1, tiled=True)  37.6 us
    all_to_all x1, waiting for transfers between devices, per_device(): lax.all_to_all(local_up_factor, ('tp', 'cores'), split_axis=1, concat_axi...  28.9 us
    unnamed x3, other arithmetic  28.6 us
    gather x4, local copies, waits for them, and re-layouts, per_device(): jnp.take(b_chosen, tile_seg, axis=0)  24.6 us
  transfers between devices with their start and end apart: 5, of which 3 were waited for; matrix products, arithmetic and copies ran while one was open for 41% of the time, Pallas kernels for 0%

commit v1 on v0

v1 whole, which is shorter than its diff:
```python
import functools

import jax
import jax.numpy as jnp
from jax import lax
from jax.experimental import pallas as pl
from jax.experimental.pallas import tpu as pltpu
from jax.sharding import PartitionSpec as P

TILE = 128
VMEM_LIMIT = 60 * 1024 * 1024

adapter_scale = 0.5

TP = ("tp", "cores")


def tile_segments(tile_lengths, tile_count):
    bounds = jnp.cumsum(tile_lengths)
    positions = jnp.arange(tile_count, dtype=jnp.int32)
    return jnp.sum((bounds[None, :] <= positions[:, None]).astype(jnp.int32), axis=1)


def ring_device(position, tp_size, cores_size):
    c = position // tp_size
    t = position % tp_size
    t = t + (c % 2) * (tp_size - 1 - 2 * t)
    return t * cores_size + c


def ring_position(tp_index, cores_index, tp_size):
    t = tp_index + (cores_index % 2) * (tp_size - 1 - 2 * tp_index)
    return cores_index * tp_size + t


def partial_kernel(count, with_acc, rows_ref, *refs):
    xs, ws = refs[:count], refs[count : 2 * count]
    out = refs[-1]
    for h in range(2):
        total = refs[2 * count][h] if with_acc else None
        for x, w in zip(xs, ws):
            term = jnp.dot(x[...], w[h], preferred_element_type=jnp.float32)
            total = term if total is None else total + term
        out[h] = total


def partial_matmul(xs, weight, rows, acc, block_cols):
    count = len(xs)
    tokens, depth = xs[0].shape
    hidden = weight.shape[2]
    block_rows = tokens // 2
    in_specs = [pl.BlockSpec((block_rows, depth), lambda j, i, r: (i, 0))] * count
    for k in range(count):
        in_specs.append(
            pl.BlockSpec((2, depth, block_cols), lambda j, i, r, k=k: (0, r[k], j))
        )
    acc_spec = pl.BlockSpec((2, block_rows, block_cols), lambda j, i, r: (0, i, j))
    operands = list(xs) + [weight] * count
    aliases = {}
    if acc is not None:
        in_specs.append(acc_spec)
        aliases = {1 + len(operands): 0}
        operands.append(acc)
    return pl.pallas_call(
        functools.partial(partial_kernel, count, acc is not None),
        out_shape=jax.ShapeDtypeStruct((2, tokens, hidden), jnp.float32),
        grid_spec=pltpu.PrefetchScalarGridSpec(
            num_scalar_prefetch=1,
            grid=(hidden // block_cols, 2),
            in_specs=in_specs,
            out_specs=acc_spec,
        ),
        input_output_aliases=aliases,
        compiler_params=pltpu.CompilerParams(vmem_limit_bytes=VMEM_LIMIT),
        cost_estimate=pl.CostEstimate(
            flops=4 * count * tokens * depth * hidden,
            bytes_accessed=count * 4 * depth * hidden + 16 * tokens * hidden,
            transcendentals=0,
        ),
    )(rows, *operands)


def final_kernel(tiles_per_block, rank, rows_ref, seg_ref, x, w, acc, shrunk, b, out, total):
    i = pl.program_id(1)
    narrow = out.shape[1]
    for h in range(2):
        total[h] = acc[h] + jnp.dot(x[...], w[h], preferred_element_type=jnp.float32)

    for t in range(tiles_per_block):
        seg = seg_ref[i * tiles_per_block + t]
        span = slice(t * TILE, (t + 1) * TILE)
        both = []
        for h in range(2):
            delta = jnp.dot(
                shrunk[span, h * rank : (h + 1) * rank],
                b[0, seg, :, h * narrow : (h + 1) * narrow],
                preferred_element_type=jnp.float32,
            )
            both.append(total[h, span] + adapter_scale * delta)
        gate, up = both
        out[span] = (gate / (1.0 + jnp.exp(-gate)) * up).astype(out.dtype)


def final_matmul(x, weight, rows, acc, shrunk, b_chosen, tile_seg):
    tokens, depth = x.shape
    hidden = weight.shape[2]
    blocks, segs, rank, twice = b_chosen.shape
    narrow = twice // 2
    block_rows = tokens // 2
    return pl.pallas_call(
        functools.partial(final_kernel, block_rows // TILE, rank),
        out_shape=jax.ShapeDtypeStruct((tokens, hidden), jnp.bfloat16),
        grid_spec=pltpu.PrefetchScalarGridSpec(
            num_scalar_prefetch=2,
            grid=(blocks, 2),
            in_specs=[
                pl.BlockSpec((block_rows, depth), lambda j, i, r, s: (i, 0)),
                pl.BlockSpec((2, depth, narrow), lambda j, i, r, s: (0, r[0], j)),
                pl.BlockSpec((2, block_rows, narrow), lambda j, i, r, s: (0, i, j)),
                pl.BlockSpec((block_rows, 2 * rank), lambda j, i, r, s: (i, 0)),
                pl.BlockSpec((1, segs, rank, twice), lambda j, i, r, s: (j, 0, 0, 0)),
            ],
            out_specs=pl.BlockSpec((block_rows, narrow), lambda j, i, r, s: (i, j)),
            scratch_shapes=[pltpu.VMEM((2, block_rows, narrow), jnp.float32)],
        ),
        compiler_params=pltpu.CompilerParams(vmem_limit_bytes=VMEM_LIMIT),
        cost_estimate=pl.CostEstimate(
            flops=4 * tokens * (depth + rank) * hidden,
            bytes_accessed=4 * depth * hidden + 10 * tokens * hidden,
            transcendentals=tokens * hidden,
        ),
    )(rows, tile_seg, x, weight, acc, shrunk, b_chosen)


def per_device(
    tokens,
    gate_up_weight,
    down_factor_pool,
    up_factor_pool,
    segment_adapters,
    segment_tile_counts,
    adapter_pool_rows,
):
    groups = lax.axis_size("grp")
    tp_size, cores_size = lax.axis_size("tp"), lax.axis_size("cores")
    n = tp_size * cores_size
    token_count, depth = tokens.shape
    local_hidden_width = gate_up_weight.shape[2]
    twice_rank = down_factor_pool.shape[2]
    narrow = local_hidden_width // groups
    seg_count = segment_adapters.shape[1]
    half = token_count // 2

    me = ring_position(lax.axis_index("tp"), lax.axis_index("cores"), tp_size)
    order = [ring_device(k, tp_size, cores_size) for k in range(n)]
    forward = [(order[k], order[(k + 1) % n]) for k in range(n)]
    backward = [(order[(k + 1) % n], order[k]) for k in range(n)]

    def owner(shift):
        return ring_device((me + shift + n) % n, tp_size, cores_size).astype(jnp.int32)

    full_steps = (n - 1) // 2
    lefts, rights = [tokens], [tokens]
    for _ in range(full_steps):
        lefts.append(lax.ppermute(lefts[-1], TP, forward))
        rights.append(lax.ppermute(rights[-1], TP, backward))
    last = jnp.concatenate(
        [
            lax.ppermute(lefts[-1][:half], TP, forward),
            lax.ppermute(rights[-1][half:], TP, backward),
        ],
        axis=0,
    )

    piece = depth // groups
    a = down_factor_pool.reshape(n // groups, groups, piece, twice_rank)
    a = lax.all_to_all(a, "grp", split_axis=1, concat_axis=0, tiled=True)
    a = a.reshape(n, piece, twice_rank)
    a = lax.all_to_all(a, TP, split_axis=0, concat_axis=0, tiled=True)
    b = up_factor_pool.reshape(up_factor_pool.shape[2:])
    b = lax.all_to_all(b, TP, split_axis=0, concat_axis=0, tiled=True)
    slots = jnp.take(adapter_pool_rows, segment_adapters.reshape(-1))
    a = jnp.take(a, slots, axis=0)
    b = jnp.take(b, slots, axis=0)
    a = lax.all_to_all(a, "grp", split_axis=0, concat_axis=0, tiled=True)
    b = lax.all_to_all(b, "grp", split_axis=0, concat_axis=0, tiled=True)
    a = a.reshape(groups, seg_count, piece, twice_rank)
    b = b.reshape(groups, seg_count, *b.shape[1:])
    block_cols = narrow
    if narrow % 128:
        block_cols = local_hidden_width
        b = b.reshape(groups, seg_count, b.shape[2], 2, narrow)
        b = jnp.transpose(b, (1, 2, 3, 0, 4))
        b = b.reshape(1, seg_count, b.shape[1], 2 * block_cols)

    tile_count = token_count // TILE
    tile_seg = tile_segments(segment_tile_counts[0], tile_count).astype(jnp.int32)
    row_seg = jnp.repeat(tile_seg, TILE)[:, None]
    partial = None
    for j in range(seg_count):
        term = jnp.dot(
            tokens, a[:, j].reshape(depth, twice_rank), preferred_element_type=jnp.float32
        )
        partial = term if partial is None else jnp.where(row_seg == j, term, partial)
    share = token_count // n
    partial = lax.all_to_all(
        partial.reshape(n, share, twice_rank), TP, split_axis=0, concat_axis=0, tiled=True
    )
    own = jnp.sum(partial, axis=0).astype(jnp.bfloat16)
    shrunk = lax.all_to_all(
        jnp.broadcast_to(own[None], (n, share, twice_rank)),
        TP,
        split_axis=0,
        concat_axis=0,
        tiled=True,
    ).reshape(token_count, twice_rank)

    weight = jnp.transpose(gate_up_weight, (1, 0, 2))
    acc = None
    for s in range(1, full_steps + 1):
        xs = [lefts[s], rights[s]]
        rows = [owner(-s), owner(s)]
        if s == 1:
            xs.insert(0, tokens)
            rows.insert(0, owner(0))
        acc = partial_matmul(xs, weight, jnp.stack(rows), acc, block_cols)
    return final_matmul(
        last, weight, jnp.stack([owner(n // 2)]), acc, shrunk, b, tile_seg
    )


def solution(mesh):
    return jax.shard_map(
        per_device,
        mesh=mesh,
        in_specs=(
            P("grp", ("tp", "cores")),
            P(None, None, ("tp", "cores")),
            P(("tp", "cores"), "grp", None),
            P(("tp", "cores"), "grp", None, None, None),
            P(),
            P("grp", None),
            P(),
        ),
        out_specs=P("grp", ("tp", "cores")),
        check_vma=False,
    )
```

time: 644 us -> 393 us (0.61); the launches traced: 635 us -> 392 us
  local copies, waits for them, and re-layouts: 299 us -> 57.6 us
  Pallas kernels: 0 us -> 126 us
  matrix products: 97.6 us -> 2.35 us
  other arithmetic: 61.6 us -> 8.83 us
  waiting for transfers between devices: 71.4 us -> 112 us
  blocking collectives: 70.2 us -> 41.8 us
  starting transfers between devices: 21.4 us -> 43.2 us
  between operations: 13.8 us -> 0.19 us
    pallas_call x0 -> x4, Pallas kernels: none -> 126 us  [the longest x3 102 us: partial_matmul(): pl.pallas_call(functools.partial(partial_kernel, count, acc is not None),...]
    dot_general x4 -> x3, matrix products: 97.6 us -> 2.35 us  [per_device(): jnp.dot(tokens, a[:, j].reshape(depth, twice_rank), preferred_element_typ...]
    dot_general x1 -> x0, local copies, waits for them, and re-layouts: 83.4 us -> none  [per_device(): jnp.dot(gathered, gate_up_weight.reshape(full_width, 2 * local_hidden_wid...]
    ppermute x0 -> x8, waiting for transfers between devices: none -> 77.3 us  [the longest x3 77.3 us: per_device(): lefts.append(lax.ppermute(lefts[-1], TP, forward))]
    psum x1 -> x0, blocking collectives: 70.2 us -> none  [per_device(): lax.psum(partial_shrink, ('tp', 'cores')).astype(jnp.bfloat16)]
    unnamed x23 -> x15, local copies, waits for them, and re-layouts: 101 us -> 44.3 us
    gather x15 -> x3, local copies, waits for them, and re-layouts: 57.4 us -> 3.64 us  [the longest x1 2.34 us: per_device(): b = jnp.take(b, slots, axis=0)]
    all_to_all x0 -> x2, blocking collectives: none -> 41.8 us  [the longest x1 23.3 us: per_device(): a = lax.all_to_all(a, 'grp', split_axis=0, concat_axis=0, tiled=True)]
  transfers between devices with their start and end apart: 5 -> 13, of which waited for: 3 -> 3; matrix products, arithmetic and copies ran while one was open for 41% -> 17% of each run, Pallas kernels for 0% -> 26%
where the time goes in v1:
time: 393 us; the launch traced here: 392 us
  Pallas kernels  126 us (32%)
  waiting for transfers between devices  112 us (28%)
  local copies, waits for them, and re-layouts  57.6 us (15%)
  starting transfers between devices  43.2 us (11%)
  blocking collectives  41.8 us (11%)
  other arithmetic  8.83 us (2%)
    pallas_call x3, Pallas kernels, partial_matmul(): pl.pallas_call(functools.partial(partial_kernel, count, acc is not None),...  102 us
    ppermute x3, waiting for transfers between devices, per_device(): lefts.append(lax.ppermute(lefts[-1], TP, forward))  77.3 us
    unnamed x15, local copies, waits for them, and re-layouts  44.3 us
    all_to_all x1, waiting for transfers between devices, per_device(): a = lax.all_to_all(a, TP, split_axis=0, concat_axis=0, tiled=True)  24.7 us
    pallas_call x1, Pallas kernels, final_matmul(): pl.pallas_call(functools.partial(final_kernel, block_rows // TILE, rank),...  23.6 us
    all_to_all x1, blocking collectives, per_device(): a = lax.all_to_all(a, 'grp', split_axis=0, concat_axis=0, tiled=True)  23.3 us
    all_to_all x1, blocking collectives, per_device(): a = lax.all_to_all(a, 'grp', split_axis=1, concat_axis=0, tiled=True)  18.6 us
    ppermute x3, starting transfers between devices, per_device(): lefts.append(lax.ppermute(lefts[-1], TP, forward))  16.7 us
  transfers between devices with their start and end apart: 13, of which 3 were waited for; matrix products, arithmetic and copies ran while one was open for 17% of the time, Pallas kernels for 26%

profile of v1, /device:TPU:0, one launch (start us, length us, event | category | flops | bytes accessed | tf_op | source)
XLA Modules:
  0.0 392.1 jit_solution(2314750997052689813)
XLA Ops:
  0.0 1.3 copy.20
  1.3 18.6 %all_to_all.45 = bf16[2,4,256,256]{3,2,0,1:T(8,128)(2,1)} all-to-all(bf16[2,4,256,256]{3,2,0,1:T(8,128)(2,1)S(1)} %copy.20), channel_id=1, replica_groups=mesh['grp'=4,'tp'=4,'cores'=2] {'grp'}, dimensions={1} | all-to-all | bytes 2097152 | tf_op jit(solution)/shard_map/all_to_all | solution.py:177
  19.9 6.3 %all-to-all-start.1 = ((bf16[8,256,256]{2,1,0:T(8,128)(2,1)}), bf16[8,256,256]{2,1,0:T(8,128)(2,1)S(1)}, u32[]{:S(2)}, u32[]{:S(2)}) async-start(bf16[8,256,256]{2,1,0:T(8,128)(2,1)} %bitcast.16), calls=%async_computation.1 | async-start | bytes 2097152 | tf_op jit(solution)/shard_map/all_to_all | solution.py:179
  27.1 24.7 %all-to-all-done.1 = bf16[8,256,256]{2,1,0:T(8,128)(2,1)S(1)} async-done(((bf16[8,256,256]{2,1,0:T(8,128)(2,1)}), bf16[8,256,256]{2,1,0:T(8,128)(2,1)S(1)}, u32[]{:S(2)}, u32[]{:S(2)}) %all-to-all-start.1) | async-done | bytes 1048608 | tf_op jit(solution)/shard_map/all_to_all | solution.py:179
  52.6 23.3 %all_to_all.46 = bf16[12,256,256]{2,1,0:T(8,128)(2,1)} all-to-all(bf16[12,256,256]{2,1,0:T(8,128)(2,1)S(1)} %broadcast_select_fusion.1), channel_id=1, replica_groups=mesh['grp'=4,'tp'=4,'cores'=2] {'grp'}, dimensions={0} | all-to-all | bytes 3145728 | tf_op jit(solution)/shard_map/all_to_all | solution.py:185
  75.9 4.5 %all-to-all-start.5 = ((bf16[8,128,1024]{2,1,0:T(8,128)(2,1)}), bf16[8,128,1024]{2,1,0:T(8,128)(2,1)}, u32[]{:S(2)}, u32[]{:S(2)}) async-start(bf16[8,128,1024]{2,1,0:T(8,128)(2,1)} %bitcast.52), calls=%async_computation.5 | async-start | bytes 4194304 | tf_op jit(solution)/shard_map/all_to_all | solution.py:181
  80.4 1.9 collective-permute-start
  82.8 77.3 %collective-permute-done.refs_1_ = bf16[1024,1024]{1,0:T(8,128)(2,1)} collective-permute-done((bf16[1024,1024]{1,0:T(8,128)(2,1)S(1)}, bf16[1024,1024]{1,0:T(8,128)(2,1)}, u32[]{:S(2)}, u32[]{:S(2)}) %collective-permute-start) | collective-permute-done | bytes 2097184 | tf_op jit(solution)/shard_map/ppermute | solution.py:165
  160.1 12.8 %collective-permute-start.1 = (bf16[1024,1024]{1,0:T(8,128)(2,1)}, bf16[1024,1024]{1,0:T(8,128)(2,1)}, u32[]{:S(2)}, u32[]{:S(2)}) collective-permute-start(bf16[1024,1024]{1,0:T(8,128)(2,1)} %collective-permute-done.refs_1_), channel_id=1, source_target_pairs={{0,2},{2,4},{4,6},{6,7},{7,5},{5,3},{3,1},{1,0},{8,10},{10,12},{12... | collective-permute-start | bytes 6291464 | tf_op jit(solution)/shard_map/ppermute | solution.py:165
  172.9 1.5 fusion.4
  174.4 0.8 fusion.5
  175.1 0.8 fusion.6
  175.9 0.8 fusion.1
  176.7 1.0 copy.29
  177.8 5.4 %all-to-all-start.3 = ((f32[8,128,256]{1,2,0:T(8,128)}), f32[8,128,256]{1,2,0:T(8,128)}, u32[]{:S(2)}, u32[]{:S(2)}) async-start(f32[8,128,256]{1,2,0:T(8,128)} %bitcast.49), calls=%async_computation.3 | async-start | bytes 2097152 | tf_op jit(solution)/shard_map/all_to_all | solution.py:206
  183.2 44.3 %copy.28 = bf16[8192,2,2048]{2,0,1:T(8,128)(2,1)} copy(bf16[8192,2,2048]{2,1,0:T(2,128)(2,1)} %param.8) | data formatting | bytes 134217728 | tf_op args[1]
  229.4 2.3 gather_fusion.2
  231.7 2.0 broadcast_select_fusion
  233.8 2.0 collective-permute-start.2
  235.8 10.4 %all-to-all-done.3 = f32[8,128,256]{1,2,0:T(8,128)} async-done(((f32[8,128,256]{1,2,0:T(8,128)}), f32[8,128,256]{1,2,0:T(8,128)}, u32[]{:S(2)}, u32[]{:S(2)}) %all-to-all-start.3) | async-done | bytes 1048608 | tf_op jit(solution)/shard_map/all_to_all | solution.py:206
  246.2 3.7 all-to-all-start.6
  250.0 37.4 %shard_map.73.refs_4_ = f32[2,1024,2048]{2,1,0:T(8,128)} custom-call(s32[3]{0:T(128)} %pad_add_fusion.2.rows_ref, bf16[1024,1024]{1,0:T(8,128)(2,1)} %refs_0_.1, bf16[1024,1024]{1,0:T(8,128)(2,1)} %collective-permute-done.refs_1_, bf16[1024,1024]{1,0:T(8,128)(2,1)} %collective-permute-done.4.refs_2_, ...), custom_call_target="tpu_custom_call" | custom-call | flops 25769803776 | bytes 58720256 | tf_op jit(solution)/shard_map/pallas_call | solution.py:64
  287.3 32.4 %shard_map.74.refs_4_ = f32[2,1024,2048]{2,1,0:T(8,128)} custom-call(s32[2]{0:T(128)} %pad_add_fusion.1.rows_ref, bf16[1024,1024]{1,0:T(8,128)(2,1)} %collective-permute-done.1.refs_0_, bf16[1024,1024]{1,0:T(8,128)(2,1)} %collective-permute-done.5.refs_1_, ...), custom_call_target="tpu_custom_call", output_to_operand_aliasing={{}: (5, {})} | custom-call | flops 17179869184 | bytes 50331648 | tf_op jit(solution)/shard_map/pallas_call | solution.py:64
  319.7 1.3 reduce_sum.19
  321.1 2.3 slice.26
  323.5 2.3 slice.27
  325.7 2.0 collective-permute-start.7
  327.8 0.9 broadcast_in_dim.54
  328.6 4.3 %all-to-all-start.4 = ((bf16[8,128,256]{2,1,0:T(8,128)(2,1)}), bf16[8,128,256]{2,1,0:T(8,128)(2,1)}, u32[]{:S(2)}, u32[]{:S(2)}) async-start(bf16[8,128,256]{2,1,0:T(8,128)(2,1)} %broadcast_in_dim.54), calls=%async_computation.4 | async-start | bytes 1048576 | tf_op jit(solution)/shard_map/all_to_all | solution.py:210
  333.0 32.4 %shard_map.75.acc = f32[2,1024,2048]{2,1,0:T(8,128)} custom-call(s32[2]{0:T(128)} %pad_add_fusion.rows_ref, bf16[1024,1024]{1,0:T(8,128)(2,1)} %collective-permute-done.2.refs_0_, bf16[1024,1024]{1,0:T(8,128)(2,1)} %collective-permute-done.6.refs_1_, ...), custom_call_target="tpu_custom_call", output_to_operand_aliasing={{}: (5, {})} | custom-call | flops 17179869184 | bytes 50331648 | tf_op jit(solution)/shard_map/pallas_call | solution.py:64
  365.4 3.1 pad_maximum_fusion.x
  368.5 23.6 %shard_map.76 = bf16[1024,2048]{1,0:T(8,128)(2,1)} custom-call(s32[1]{0:T(128)} %bitcast.rows_ref, s32[8]{0:T(128)} %copy-done.5, bf16[1024,1024]{1,0:T(8,128)(2,1)} %pad_maximum_fusion.x, bf16[2,8192,2048]{2,1,0:T(8,128)(2,1)} %bitcast.48.refs_3_.refs_4_.refs_5_.refs_2_.w, f32[2,1024,2048]{2,1,0:T(8,128)} %shard_map.75.acc, ...), custom_call_target="tpu_custom_call" | custom-call | flops 9663676416 | bytes 29360128 | tf_op jit(solution)/shard_map/pallas_call | solution.py:110
  (46 shorter events, 4.4 us)
Async XLA Ops:
  0.0 26.4 %copy-start = (s32[8]{0:T(128)S(1)}, s32[8]{0:T(128)}, u32[]{:S(2)}) copy-start(s32[8]{0:T(128)} %param.13) | copy-start | bytes 100
  1.3 24.9 %copy-start.4 = (s32[4,3]{1,0:T(4,128)S(1)}, s32[4,3]{1,0:T(4,128)}, u32[]{:S(2)}) copy-start(s32[4,3]{1,0:T(4,128)} %param.11) | copy-start | bytes 148
  19.9 31.9 %all-to-all-start.1 = ((bf16[8,256,256]{2,1,0:T(8,128)(2,1)}), bf16[8,256,256]{2,1,0:T(8,128)(2,1)S(1)}, u32[]{:S(2)}, u32[]{:S(2)}) async-start(bf16[8,256,256]{2,1,0:T(8,128)(2,1)} %bitcast.16), calls=%async_computation.1 | async-start | bytes 2097152 | tf_op jit(solution)/shard_map/all_to_all | solution.py:179
  75.9 4.5 %copy-start.2 = (bf16[1024,1024]{1,0:T(8,128)(2,1)S(1)}, bf16[1024,1024]{1,0:T(8,128)(2,1)}, u32[]{:S(2)}) copy-start(bf16[1024,1024]{1,0:T(8,128)(2,1)} %refs_0_.1) | copy-start | bytes 6291460
  75.9 6.6 %copy-start.6 = (s32[1,3]{1,0:T(1,128)S(1)}, s32[1,3]{1,0:T(1,128)}, u32[]{:S(2)}) copy-start(s32[1,3]{1,0:T(1,128)} %param.12) | copy-start | bytes 40
  75.9 101.9 %all-to-all-start.5 = ((bf16[8,128,1024]{2,1,0:T(8,128)(2,1)}), bf16[8,128,1024]{2,1,0:T(8,128)(2,1)}, u32[]{:S(2)}, u32[]{:S(2)}) async-start(bf16[8,128,1024]{2,1,0:T(8,128)(2,1)} %bitcast.52), calls=%async_computation.5 | async-start | bytes 4194304 | tf_op jit(solution)/shard_map/all_to_all | solution.py:181
  80.4 79.7 %collective-permute-start = (bf16[1024,1024]{1,0:T(8,128)(2,1)S(1)}, bf16[1024,1024]{1,0:T(8,128)(2,1)}, u32[]{:S(2)}, u32[]{:S(2)}) collective-permute-start(bf16[1024,1024]{1,0:T(8,128)(2,1)S(1)} %copy-done.2), channel_id=1, source_target_pairs={{0,2},{2,4},{4,6},{6,7},{7,5},{5,3},{3,1},{1,0},{8,10},{10,12},{12... | collective-permute-start | bytes 6291464 | tf_op jit(solution)/shard_map/ppermute | solution.py:165
  82.3 90.6 %collective-permute-start.4 = (bf16[1024,1024]{1,0:T(8,128)(2,1)S(1)}, bf16[1024,1024]{1,0:T(8,128)(2,1)}, u32[]{:S(2)}, u32[]{:S(2)}) collective-permute-start(bf16[1024,1024]{1,0:T(8,128)(2,1)S(1)} %copy-done.2), channel_id=1, source_target_pairs={{2,0},{4,2},{6,4},{7,6},{5,7},{3,5},{1,3},{0,1},{10,8},{12,10},{14... | collective-permute-start | bytes 6291464 | tf_op jit(solution)/shard_map/ppermute | solution.py:166
  82.7 92.4 %copy-start.5 = (s32[8]{0:T(128)}, s32[8]{0:T(128)S(1)}, u32[]{:S(2)}) copy-start(s32[8]{0:T(128)S(1)} %convert_reduce_fusion.seg_ref) | copy-start | bytes 100
  160.1 73.7 %collective-permute-start.1 = (bf16[1024,1024]{1,0:T(8,128)(2,1)}, bf16[1024,1024]{1,0:T(8,128)(2,1)}, u32[]{:S(2)}, u32[]{:S(2)}) collective-permute-start(bf16[1024,1024]{1,0:T(8,128)(2,1)} %collective-permute-done.refs_1_), channel_id=1, source_target_pairs={{0,2},{2,4},{4,6},{6,7},{7,5},{5,3},{3,1},{1,0},{8,10},{10,12},{12... | collective-permute-start | bytes 6291464 | tf_op jit(solution)/shard_map/ppermute | solution.py:165
  172.9 62.9 %collective-permute-start.5 = (bf16[1024,1024]{1,0:T(8,128)(2,1)}, bf16[1024,1024]{1,0:T(8,128)(2,1)}, u32[]{:S(2)}, u32[]{:S(2)}) collective-permute-start(bf16[1024,1024]{1,0:T(8,128)(2,1)} %collective-permute-done.4.refs_2_), channel_id=1, source_target_pairs={{2,0},{4,2},{6,4},{7,6},{5,7},{3,5},{1,3},{0,1},{10,8},{12,10},{14... | collective-permute-start | bytes 6291464 | tf_op jit(solution)/shard_map/ppermute | solution.py:166
  177.8 68.4 %all-to-all-start.3 = ((f32[8,128,256]{1,2,0:T(8,128)}), f32[8,128,256]{1,2,0:T(8,128)}, u32[]{:S(2)}, u32[]{:S(2)}) async-start(f32[8,128,256]{1,2,0:T(8,128)} %bitcast.49), calls=%async_computation.3 | async-start | bytes 2097152 | tf_op jit(solution)/shard_map/all_to_all | solution.py:206
  233.8 87.4 %collective-permute-start.2 = (bf16[1024,1024]{1,0:T(8,128)(2,1)}, bf16[1024,1024]{1,0:T(8,128)(2,1)}, u32[]{:S(2)}, u32[]{:S(2)}) collective-permute-start(bf16[1024,1024]{1,0:T(8,128)(2,1)} %collective-permute-done.1.refs_0_), channel_id=1, source_target_pairs={{0,2},{2,4},{4,6},{6,7},{7,5},{5,3},{3,1},{1,0},{8,10},{10,12},{12... | collective-permute-start | bytes 6291464 | tf_op jit(solution)/shard_map/ppermute | solution.py:165
  235.8 87.7 %collective-permute-start.6 = (bf16[1024,1024]{1,0:T(8,128)(2,1)}, bf16[1024,1024]{1,0:T(8,128)(2,1)}, u32[]{:S(2)}, u32[]{:S(2)}) collective-permute-start(bf16[1024,1024]{1,0:T(8,128)(2,1)} %collective-permute-done.5.refs_1_), channel_id=1, source_target_pairs={{2,0},{4,2},{6,4},{7,6},{5,7},{3,5},{1,3},{0,1},{10,8},{12,10},{14... | collective-permute-start | bytes 6291464 | tf_op jit(solution)/shard_map/ppermute | solution.py:166
  246.2 81.5 %all-to-all-start.6 = ((bf16[12,128,1024]{2,1,0:T(8,128)(2,1)}), bf16[12,128,1024]{2,1,0:T(8,128)(2,1)S(1)}, u32[]{:S(2)}, u32[]{:S(2)}) async-start(bf16[12,128,1024]{2,1,0:T(8,128)(2,1)} %broadcast_select_fusion), calls=%async_computation.6 | async-start | bytes 6291456 | tf_op jit(solution)/shard_map/all_to_all | solution.py:186
  323.5 41.9 %collective-permute-start.3 = (bf16[512,1024]{1,0:T(8,128)(2,1)}, bf16[512,1024]{1,0:T(8,128)(2,1)}, u32[]{:S(2)}, u32[]{:S(2)}) collective-permute-start(bf16[512,1024]{1,0:T(8,128)(2,1)} %slice.26), channel_id=1, source_target_pairs={{0,2},{2,4},{4,6},{6,7},{7,5},{5,3},{3,1},{1,0},{8,10},{10,12},{12... | collective-permute-start | bytes 3145736 | tf_op jit(solution)/shard_map/ppermute | solution.py:169
  325.7 39.7 %collective-permute-start.7 = (bf16[512,1024]{1,0:T(8,128)(2,1)}, bf16[512,1024]{1,0:T(8,128)(2,1)}, u32[]{:S(2)}, u32[]{:S(2)}) collective-permute-start(bf16[512,1024]{1,0:T(8,128)(2,1)} %slice.27), channel_id=1, source_target_pairs={{2,0},{4,2},{6,4},{7,6},{5,7},{3,5},{1,3},{0,1},{10,8},{12,10},{14... | collective-permute-start | bytes 3145736 | tf_op jit(solution)/shard_map/ppermute | solution.py:170
  327.8 37.6 %copy-start.3 = (bf16[12,128,1024]{2,1,0:T(8,128)(2,1)}, bf16[12,128,1024]{2,1,0:T(8,128)(2,1)S(1)}, u32[]{:S(2)}) copy-start(bf16[12,128,1024]{2,1,0:T(8,128)(2,1)S(1)} %all-to-all-done.6) | copy-start | bytes 9437188
  328.6 39.8 %all-to-all-start.4 = ((bf16[8,128,256]{2,1,0:T(8,128)(2,1)}), bf16[8,128,256]{2,1,0:T(8,128)(2,1)}, u32[]{:S(2)}, u32[]{:S(2)}) async-start(bf16[8,128,256]{2,1,0:T(8,128)(2,1)} %broadcast_in_dim.54), calls=%async_computation.4 | async-start | bytes 1048576 | tf_op jit(solution)/shard_map/all_to_all | solution.py:210
  368.5 23.6 %copy-start.1 = (s32[8]{0:T(128)S(1)}, s32[8]{0:T(128)}, u32[]{:S(2)}) copy-start(s32[8]{0:T(128)} %param.13) | copy-start | bytes 100

commit v2 on v1

--- a/solution.py
+++ b/solution.py
@@ -6,6 +6,7 @@
 from jax.experimental import pallas as pl
 from jax.experimental.pallas import tpu as pltpu
 from jax.sharding import PartitionSpec as P
+
 
 TILE = 128
 VMEM_LIMIT = 60 * 1024 * 1024
@@ -48,13 +49,13 @@
     count = len(xs)
     tokens, depth = xs[0].shape
     hidden = weight.shape[2]
-    block_rows = tokens // 2
-    in_specs = [pl.BlockSpec((block_rows, depth), lambda j, i, r: (i, 0))] * count
+    block_cols = min(block_cols, 256)
+    in_specs = [pl.BlockSpec((tokens, depth), lambda j, r: (0, 0))] * count
     for k in range(count):
         in_specs.append(
-            pl.BlockSpec((2, depth, block_cols), lambda j, i, r, k=k: (0, r[k], j))
+            pl.BlockSpec((2, depth, block_cols), lambda j, r, k=k: (0, r[k], j))
         )
-    acc_spec = pl.BlockSpec((2, block_rows, block_cols), lambda j, i, r: (0, i, j))
+    acc_spec = pl.BlockSpec((2, tokens, block_cols), lambda j, r: (0, 0, j))
     operands = list(xs) + [weight] * count
     aliases = {}
     if acc is not None:
@@ -66,7 +67,7 @@
         out_shape=jax.ShapeDtypeStruct((2, tokens, hidden), jnp.float32),
         grid_spec=pltpu.PrefetchScalarGridSpec(
             num_scalar_prefetch=1,
-            grid=(hidden // block_cols, 2),
+            grid=(hidden // block_cols,),
             in_specs=in_specs,
             out_specs=acc_spec,
         ),
@@ -80,48 +81,51 @@
     )(rows, *operands)
 
 
-def final_kernel(tiles_per_block, rank, rows_ref, seg_ref, x, w, acc, shrunk, b, out, total):
-    i = pl.program_id(1)
+def final_kernel(tiles_per_half, rank, rows_ref, seg_ref, xt, xb, w, acc, shrunk, b, out, total):
     narrow = out.shape[1]
-    for h in range(2):
-        total[h] = acc[h] + jnp.dot(x[...], w[h], preferred_element_type=jnp.float32)
-
-    for t in range(tiles_per_block):
-        seg = seg_ref[i * tiles_per_block + t]
-        span = slice(t * TILE, (t + 1) * TILE)
-        both = []
+    for p, x in enumerate((xt, xb)):
         for h in range(2):
-            delta = jnp.dot(
-                shrunk[span, h * rank : (h + 1) * rank],
-                b[0, seg, :, h * narrow : (h + 1) * narrow],
-                preferred_element_type=jnp.float32,
+            span = slice(p * x.shape[0], (p + 1) * x.shape[0])
+            total[h, span] = acc[h, span] + jnp.dot(
+                x[...], w[h], preferred_element_type=jnp.float32
             )
-            both.append(total[h, span] + adapter_scale * delta)
-        gate, up = both
-        out[span] = (gate / (1.0 + jnp.exp(-gate)) * up).astype(out.dtype)
-
-
-def final_matmul(x, weight, rows, acc, shrunk, b_chosen, tile_seg):
-    tokens, depth = x.shape
+        for t in range(p * tiles_per_half, (p + 1) * tiles_per_half):
+            seg = seg_ref[t]
+            span = slice(t * TILE, (t + 1) * TILE)
+            both = []
+            for h in range(2):
+                delta = jnp.dot(
+                    shrunk[span, h * rank : (h + 1) * rank],
+                    b[0, seg, :, h * narrow : (h + 1) * narrow],
+                    preferred_element_type=jnp.float32,
+                )
+                both.append(total[h, span] + adapter_scale * delta)
+            gate, up = both
+            out[span] = (gate / (1.0 + jnp.exp(-gate)) * up).astype(out.dtype)
+
+
+def final_matmul(xt, xb, weight, rows, acc, shrunk, b_chosen, tile_seg):
+    half, depth = xt.shape
+    tokens = 2 * half
     hidden = weight.shape[2]
     blocks, segs, rank, twice = b_chosen.shape
     narrow = twice // 2
-    block_rows = tokens // 2
     return pl.pallas_call(
-        functools.partial(final_kernel, block_rows // TILE, rank),
+        functools.partial(final_kernel, half // TILE, rank),
         out_shape=jax.ShapeDtypeStruct((tokens, hidden), jnp.bfloat16),
         grid_spec=pltpu.PrefetchScalarGridSpec(
             num_scalar_prefetch=2,
-            grid=(blocks, 2),
+            grid=(blocks,),
             in_specs=[
-                pl.BlockSpec((block_rows, depth), lambda j, i, r, s: (i, 0)),
-                pl.BlockSpec((2, depth, narrow), lambda j, i, r, s: (0, r[0], j)),
-                pl.BlockSpec((2, block_rows, narrow), lambda j, i, r, s: (0, i, j)),
-                pl.BlockSpec((block_rows, 2 * rank), lambda j, i, r, s: (i, 0)),
-                pl.BlockSpec((1, segs, rank, twice), lambda j, i, r, s: (j, 0, 0, 0)),
+                pl.BlockSpec((half, depth), lambda j, r, s: (0, 0)),
+                pl.BlockSpec((half, depth), lambda j, r, s: (0, 0)),
+                pl.BlockSpec((2, depth, narrow), lambda j, r, s: (0, r[0], j)),
+                pl.BlockSpec((2, tokens, narrow), lambda j, r, s: (0, 0, j)),
+                pl.BlockSpec((tokens, 2 * rank), lambda j, r, s: (0, 0)),
+                pl.BlockSpec((1, segs, rank, twice), lambda j, r, s: (j, 0, 0, 0)),
             ],
-            out_specs=pl.BlockSpec((block_rows, narrow), lambda j, i, r, s: (i, j)),
-            scratch_shapes=[pltpu.VMEM((2, block_rows, narrow), jnp.float32)],
+            out_specs=pl.BlockSpec((tokens, narrow), lambda j, r, s: (0, j)),
+            scratch_shapes=[pltpu.VMEM((2, tokens, narrow), jnp.float32)],
         ),
         compiler_params=pltpu.CompilerParams(vmem_limit_bytes=VMEM_LIMIT),
         cost_estimate=pl.CostEstimate(
@@ -129,10 +133,10 @@
             bytes_accessed=4 * depth * hidden + 10 * tokens * hidden,
             transcendentals=tokens * hidden,
         ),
-    )(rows, tile_seg, x, weight, acc, shrunk, b_chosen)
-
-
-def per_device(
+    )(rows, tile_seg, xt, xb, weight, acc, shrunk, b_chosen)
+
+
+def compute(
     tokens,
     gate_up_weight,
     down_factor_pool,
@@ -161,16 +165,11 @@
 
     full_steps = (n - 1) // 2
     lefts, rights = [tokens], [tokens]
-    for _ in range(full_steps):
+    for _ in range(1, full_steps + 1):
         lefts.append(lax.ppermute(lefts[-1], TP, forward))
         rights.append(lax.ppermute(rights[-1], TP, backward))
-    last = jnp.concatenate(
-        [
-            lax.ppermute(lefts[-1][:half], TP, forward),
-            lax.ppermute(rights[-1][half:], TP, backward),
-        ],
-        axis=0,
-    )
+    last_top = lax.ppermute(lefts[-1][:half], TP, forward)
+    last_bottom = lax.ppermute(rights[-1][half:], TP, backward)
 
     piece = depth // groups
     a = down_factor_pool.reshape(n // groups, groups, piece, twice_rank)
@@ -225,13 +224,13 @@
             rows.insert(0, owner(0))
         acc = partial_matmul(xs, weight, jnp.stack(rows), acc, block_cols)
     return final_matmul(
-        last, weight, jnp.stack([owner(n // 2)]), acc, shrunk, b, tile_seg
+        last_top, last_bottom, weight, jnp.stack([owner(n // 2)]), acc, shrunk, b, tile_seg
     )
 
 
 def solution(mesh):
     return jax.shard_map(
-        per_device,
+        compute,
         mesh=mesh,
         in_specs=(
             P("grp", ("tp", "cores")),

time: 393 us -> 374 us (0.952)
  Pallas kernels: 126 us -> 107 us
    pallas_call x3, Pallas kernels: 102 us -> 87 us  [partial_matmul(): pl.pallas_call(functools.partial(partial_kernel, count, acc is not None),...]
  transfers between devices with their start and end apart: 13 -> 13, of which waited for: 3 -> 4; matrix products, arithmetic and copies ran while one was open for 17% -> 17% of each run, Pallas kernels for 26% -> 23%
where the time goes in v2:
time: 374 us; the launch traced here: 373 us
  waiting for transfers between devices  115 us (31%)
  Pallas kernels  107 us (29%)
  local copies, waits for them, and re-layouts  57.5 us (15%)
  starting transfers between devices  43.2 us (12%)
  blocking collectives  41.8 us (11%)
  other arithmetic  5.75 us (2%)
    pallas_call x3, Pallas kernels, partial_matmul(): pl.pallas_call(functools.partial(partial_kernel, count, acc is not None),...  87 us
    ppermute x3, waiting for transfers between devices, compute(): lefts.append(lax.ppermute(lefts[-1], TP, forward))  77.3 us
    unnamed x15, local copies, waits for them, and re-layouts  44.3 us
    all_to_all x1, waiting for transfers between devices, compute(): a = lax.all_to_all(a, TP, split_axis=0, concat_axis=0, tiled=True)  24.7 us
    all_to_all x1, blocking collectives, compute(): a = lax.all_to_all(a, 'grp', split_axis=0, concat_axis=0, tiled=True)  23.3 us
    pallas_call x1, Pallas kernels, final_matmul(): pl.pallas_call(functools.partial(final_kernel, half // TILE, rank), out_s...  20.4 us
    all_to_all x1, blocking collectives, compute(): a = lax.all_to_all(a, 'grp', split_axis=1, concat_axis=0, tiled=True)  18.6 us
    ppermute x3, starting transfers between devices, compute(): lefts.append(lax.ppermute(lefts[-1], TP, forward))  16.7 us
  transfers between devices with their start and end apart: 13, of which 4 were waited for; matrix products, arithmetic and copies ran while one was open for 17% of the time, Pallas kernels for 23%

profile of v2, /device:TPU:0, one launch (start us, length us, event | category | flops | bytes accessed | tf_op | source)
XLA Modules:
  0.0 373.1 jit_solution(5725393097156360990)
XLA Ops:
  0.0 1.3 copy.20
  1.3 18.6 %all_to_all.45 = bf16[2,4,256,256]{3,2,0,1:T(8,128)(2,1)} all-to-all(bf16[2,4,256,256]{3,2,0,1:T(8,128)(2,1)S(1)} %copy.20), channel_id=1, replica_groups=mesh['grp'=4,'tp'=4,'cores'=2] {'grp'}, dimensions={1} | all-to-all | bytes 2097152 | tf_op jit(solution)/shard_map/all_to_all | solution.py:176
  19.9 6.3 %all-to-all-start.1 = ((bf16[8,256,256]{2,1,0:T(8,128)(2,1)}), bf16[8,256,256]{2,1,0:T(8,128)(2,1)S(1)}, u32[]{:S(2)}, u32[]{:S(2)}) async-start(bf16[8,256,256]{2,1,0:T(8,128)(2,1)} %bitcast.16), calls=%async_computation.1 | async-start | bytes 2097152 | tf_op jit(solution)/shard_map/all_to_all | solution.py:178
  27.1 24.7 %all-to-all-done.1 = bf16[8,256,256]{2,1,0:T(8,128)(2,1)S(1)} async-done(((bf16[8,256,256]{2,1,0:T(8,128)(2,1)}), bf16[8,256,256]{2,1,0:T(8,128)(2,1)S(1)}, u32[]{:S(2)}, u32[]{:S(2)}) %all-to-all-start.1) | async-done | bytes 1048608 | tf_op jit(solution)/shard_map/all_to_all | solution.py:178
  52.6 23.3 %all_to_all.46 = bf16[12,256,256]{2,1,0:T(8,128)(2,1)} all-to-all(bf16[12,256,256]{2,1,0:T(8,128)(2,1)S(1)} %broadcast_select_fusion.1), channel_id=1, replica_groups=mesh['grp'=4,'tp'=4,'cores'=2] {'grp'}, dimensions={0} | all-to-all | bytes 3145728 | tf_op jit(solution)/shard_map/all_to_all | solution.py:184
  75.9 4.5 %all-to-all-start.5 = ((bf16[8,128,1024]{2,1,0:T(8,128)(2,1)}), bf16[8,128,1024]{2,1,0:T(8,128)(2,1)}, u32[]{:S(2)}, u32[]{:S(2)}) async-start(bf16[8,128,1024]{2,1,0:T(8,128)(2,1)} %bitcast.52), calls=%async_computation.5 | async-start | bytes 4194304 | tf_op jit(solution)/shard_map/all_to_all | solution.py:180
  80.4 1.9 collective-permute-start
  82.8 77.3 %collective-permute-done.refs_1_ = bf16[1024,1024]{1,0:T(8,128)(2,1)} collective-permute-done((bf16[1024,1024]{1,0:T(8,128)(2,1)S(1)}, bf16[1024,1024]{1,0:T(8,128)(2,1)}, u32[]{:S(2)}, u32[]{:S(2)}) %collective-permute-start) | collective-permute-done | bytes 2097184 | tf_op jit(solution)/shard_map/ppermute | solution.py:169
  160.1 12.8 %collective-permute-start.1 = (bf16[1024,1024]{1,0:T(8,128)(2,1)}, bf16[1024,1024]{1,0:T(8,128)(2,1)}, u32[]{:S(2)}, u32[]{:S(2)}) collective-permute-start(bf16[1024,1024]{1,0:T(8,128)(2,1)} %collective-permute-done.refs_1_), channel_id=1, source_target_pairs={{0,2},{2,4},{4,6},{6,7},{7,5},{5,3},{3,1},{1,0},{8,10},{10,12},{12... | collective-permute-start | bytes 6291464 | tf_op jit(solution)/shard_map/ppermute | solution.py:169
  172.9 1.5 fusion.4
  174.4 0.8 fusion.5
  175.1 0.8 fusion.6
  175.9 0.8 fusion.1
  176.7 1.0 copy.29
  177.8 5.4 %all-to-all-start.3 = ((f32[8,128,256]{1,2,0:T(8,128)}), f32[8,128,256]{1,2,0:T(8,128)}, u32[]{:S(2)}, u32[]{:S(2)}) async-start(f32[8,128,256]{1,2,0:T(8,128)} %bitcast.49), calls=%async_computation.3 | async-start | bytes 2097152 | tf_op jit(solution)/shard_map/all_to_all | solution.py:205
  183.2 44.3 %copy.28 = bf16[8192,2,2048]{2,0,1:T(8,128)(2,1)} copy(bf16[8192,2,2048]{2,1,0:T(2,128)(2,1)} %param.8) | data formatting | bytes 134217728 | tf_op args[1]
  229.4 2.3 gather_fusion.2
  231.7 2.0 broadcast_select_fusion
  233.8 2.0 collective-permute-start.2
  235.8 10.4 %all-to-all-done.3 = f32[8,128,256]{1,2,0:T(8,128)} async-done(((f32[8,128,256]{1,2,0:T(8,128)}), f32[8,128,256]{1,2,0:T(8,128)}, u32[]{:S(2)}, u32[]{:S(2)}) %all-to-all-start.3) | async-done | bytes 1048608 | tf_op jit(solution)/shard_map/all_to_all | solution.py:205
  246.2 3.7 all-to-all-start.6
  250.0 33.6 %shard_map.73.refs_4_ = f32[2,1024,2048]{2,1,0:T(8,128)} custom-call(s32[3]{0:T(128)} %pad_add_fusion.2.rows_ref, bf16[1024,1024]{1,0:T(8,128)(2,1)} %refs_0_.1, bf16[1024,1024]{1,0:T(8,128)(2,1)} %collective-permute-done.refs_1_, bf16[1024,1024]{1,0:T(8,128)(2,1)} %collective-permute-done.4.refs_2_, ...), custom_call_target="tpu_custom_call" | custom-call | flops 25769803776 | bytes 58720256 | tf_op jit(solution)/shard_map/pallas_call | solution.py:65
  283.5 26.7 %shard_map.74.refs_4_ = f32[2,1024,2048]{2,1,0:T(8,128)} custom-call(s32[2]{0:T(128)} %pad_add_fusion.1.rows_ref, bf16[1024,1024]{1,0:T(8,128)(2,1)} %collective-permute-done.1.refs_0_, bf16[1024,1024]{1,0:T(8,128)(2,1)} %collective-permute-done.5.refs_1_, ...), custom_call_target="tpu_custom_call", output_to_operand_aliasing={{}: (5, {})} | custom-call | flops 17179869184 | bytes 50331648 | tf_op jit(solution)/shard_map/pallas_call | solution.py:65
  310.3 1.3 reduce_sum.19
  311.7 2.3 slice.26
  313.9 2.3 slice.27
  316.2 2.0 collective-permute-start.7
  318.2 0.9 broadcast_in_dim.54
  319.1 4.3 %all-to-all-start.4 = ((bf16[8,128,256]{2,1,0:T(8,128)(2,1)}), bf16[8,128,256]{2,1,0:T(8,128)(2,1)}, u32[]{:S(2)}, u32[]{:S(2)}) async-start(bf16[8,128,256]{2,1,0:T(8,128)(2,1)} %broadcast_in_dim.54), calls=%async_computation.4 | async-start | bytes 1048576 | tf_op jit(solution)/shard_map/all_to_all | solution.py:209
  323.4 26.7 %shard_map.75.acc = f32[2,1024,2048]{2,1,0:T(8,128)} custom-call(s32[2]{0:T(128)} %pad_add_fusion.rows_ref, bf16[1024,1024]{1,0:T(8,128)(2,1)} %collective-permute-done.2.refs_0_, bf16[1024,1024]{1,0:T(8,128)(2,1)} %collective-permute-done.6.refs_1_, ...), custom_call_target="tpu_custom_call", output_to_operand_aliasing={{}: (5, {})} | custom-call | flops 17179869184 | bytes 50331648 | tf_op jit(solution)/shard_map/pallas_call | solution.py:65
  350.2 2.5 all-to-all-done.4
  352.7 20.4 %shard_map.76 = bf16[1024,2048]{1,0:T(8,128)(2,1)} custom-call(s32[1]{0:T(128)} %bitcast.rows_ref, s32[8]{0:T(128)} %copy-done.5, bf16[512,1024]{1,0:T(8,128)(2,1)} %collective-permute-done.3.xt, bf16[512,1024]{1,0:T(8,128)(2,1)} %collective-permute-done.7.xb, bf16[2,8192,2048]{2,1,0:T(8,128)(2,1)} %bitcast.48.refs_3_.refs_4_.refs_5_.refs_2_.w, ...), custom_call_target="tpu_custom_call" | custom-call | flops 9663676416 | bytes 29360128 | tf_op jit(solution)/shard_map/pallas_call | solution.py:113
  (45 shorter events, 4.4 us)
Async XLA Ops:
  0.0 26.4 %copy-start = (s32[8]{0:T(128)S(1)}, s32[8]{0:T(128)}, u32[]{:S(2)}) copy-start(s32[8]{0:T(128)} %param.13) | copy-start | bytes 100
  1.3 24.9 %copy-start.4 = (s32[4,3]{1,0:T(4,128)S(1)}, s32[4,3]{1,0:T(4,128)}, u32[]{:S(2)}) copy-start(s32[4,3]{1,0:T(4,128)} %param.11) | copy-start | bytes 148
  19.9 31.9 %all-to-all-start.1 = ((bf16[8,256,256]{2,1,0:T(8,128)(2,1)}), bf16[8,256,256]{2,1,0:T(8,128)(2,1)S(1)}, u32[]{:S(2)}, u32[]{:S(2)}) async-start(bf16[8,256,256]{2,1,0:T(8,128)(2,1)} %bitcast.16), calls=%async_computation.1 | async-start | bytes 2097152 | tf_op jit(solution)/shard_map/all_to_all | solution.py:178
  75.9 4.5 %copy-start.2 = (bf16[1024,1024]{1,0:T(8,128)(2,1)S(1)}, bf16[1024,1024]{1,0:T(8,128)(2,1)}, u32[]{:S(2)}) copy-start(bf16[1024,1024]{1,0:T(8,128)(2,1)} %refs_0_.1) | copy-start | bytes 6291460
  75.9 6.6 %copy-start.6 = (s32[1,3]{1,0:T(1,128)S(1)}, s32[1,3]{1,0:T(1,128)}, u32[]{:S(2)}) copy-start(s32[1,3]{1,0:T(1,128)} %param.12) | copy-start | bytes 40
  75.9 101.9 %all-to-all-start.5 = ((bf16[8,128,1024]{2,1,0:T(8,128)(2,1)}), bf16[8,128,1024]{2,1,0:T(8,128)(2,1)}, u32[]{:S(2)}, u32[]{:S(2)}) async-start(bf16[8,128,1024]{2,1,0:T(8,128)(2,1)} %bitcast.52), calls=%async_computation.5 | async-start | bytes 4194304 | tf_op jit(solution)/shard_map/all_to_all | solution.py:180
  80.4 79.7 %collective-permute-start = (bf16[1024,1024]{1,0:T(8,128)(2,1)S(1)}, bf16[1024,1024]{1,0:T(8,128)(2,1)}, u32[]{:S(2)}, u32[]{:S(2)}) collective-permute-start(bf16[1024,1024]{1,0:T(8,128)(2,1)S(1)} %copy-done.2), channel_id=1, source_target_pairs={{0,2},{2,4},{4,6},{6,7},{7,5},{5,3},{3,1},{1,0},{8,10},{10,12},{12... | collective-permute-start | bytes 6291464 | tf_op jit(solution)/shard_map/ppermute | solution.py:169
  82.3 90.6 %collective-permute-start.4 = (bf16[1024,1024]{1,0:T(8,128)(2,1)S(1)}, bf16[1024,1024]{1,0:T(8,128)(2,1)}, u32[]{:S(2)}, u32[]{:S(2)}) collective-permute-start(bf16[1024,1024]{1,0:T(8,128)(2,1)S(1)} %copy-done.2), channel_id=1, source_target_pairs={{2,0},{4,2},{6,4},{7,6},{5,7},{3,5},{1,3},{0,1},{10,8},{12,10},{14... | collective-permute-start | bytes 6291464 | tf_op jit(solution)/shard_map/ppermute | solution.py:170
  82.7 92.4 %copy-start.5 = (s32[8]{0:T(128)}, s32[8]{0:T(128)S(1)}, u32[]{:S(2)}) copy-start(s32[8]{0:T(128)S(1)} %convert_reduce_fusion.seg_ref) | copy-start | bytes 100
  160.1 73.7 %collective-permute-start.1 = (bf16[1024,1024]{1,0:T(8,128)(2,1)}, bf16[1024,1024]{1,0:T(8,128)(2,1)}, u32[]{:S(2)}, u32[]{:S(2)}) collective-permute-start(bf16[1024,1024]{1,0:T(8,128)(2,1)} %collective-permute-done.refs_1_), channel_id=1, source_target_pairs={{0,2},{2,4},{4,6},{6,7},{7,5},{5,3},{3,1},{1,0},{8,10},{10,12},{12... | collective-permute-start | bytes 6291464 | tf_op jit(solution)/shard_map/ppermute | solution.py:169
  172.9 62.9 %collective-permute-start.5 = (bf16[1024,1024]{1,0:T(8,128)(2,1)}, bf16[1024,1024]{1,0:T(8,128)(2,1)}, u32[]{:S(2)}, u32[]{:S(2)}) collective-permute-start(bf16[1024,1024]{1,0:T(8,128)(2,1)} %collective-permute-done.4.refs_2_), channel_id=1, source_target_pairs={{2,0},{4,2},{6,4},{7,6},{5,7},{3,5},{1,3},{0,1},{10,8},{12,10},{14... | collective-permute-start | bytes 6291464 | tf_op jit(solution)/shard_map/ppermute | solution.py:170
  177.8 68.4 %all-to-all-start.3 = ((f32[8,128,256]{1,2,0:T(8,128)}), f32[8,128,256]{1,2,0:T(8,128)}, u32[]{:S(2)}, u32[]{:S(2)}) async-start(f32[8,128,256]{1,2,0:T(8,128)} %bitcast.49), calls=%async_computation.3 | async-start | bytes 2097152 | tf_op jit(solution)/shard_map/all_to_all | solution.py:205
  233.8 77.9 %collective-permute-start.2 = (bf16[1024,1024]{1,0:T(8,128)(2,1)}, bf16[1024,1024]{1,0:T(8,128)(2,1)}, u32[]{:S(2)}, u32[]{:S(2)}) collective-permute-start(bf16[1024,1024]{1,0:T(8,128)(2,1)} %collective-permute-done.1.refs_0_), channel_id=1, source_target_pairs={{0,2},{2,4},{4,6},{6,7},{7,5},{5,3},{3,1},{1,0},{8,10},{10,12},{12... | collective-permute-start | bytes 6291464 | tf_op jit(solution)/shard_map/ppermute | solution.py:169
  235.8 78.2 %collective-permute-start.6 = (bf16[1024,1024]{1,0:T(8,128)(2,1)}, bf16[1024,1024]{1,0:T(8,128)(2,1)}, u32[]{:S(2)}, u32[]{:S(2)}) collective-permute-start(bf16[1024,1024]{1,0:T(8,128)(2,1)} %collective-permute-done.5.refs_1_), channel_id=1, source_target_pairs={{2,0},{4,2},{6,4},{7,6},{5,7},{3,5},{1,3},{0,1},{10,8},{12,10},{14... | collective-permute-start | bytes 6291464 | tf_op jit(solution)/shard_map/ppermute | solution.py:170
  246.2 72.0 %all-to-all-start.6 = ((bf16[12,128,1024]{2,1,0:T(8,128)(2,1)}), bf16[12,128,1024]{2,1,0:T(8,128)(2,1)S(1)}, u32[]{:S(2)}, u32[]{:S(2)}) async-start(bf16[12,128,1024]{2,1,0:T(8,128)(2,1)} %broadcast_select_fusion), calls=%async_computation.6 | async-start | bytes 6291456 | tf_op jit(solution)/shard_map/all_to_all | solution.py:185
  313.9 38.8 %collective-permute-start.3 = (bf16[512,1024]{1,0:T(8,128)(2,1)}, bf16[512,1024]{1,0:T(8,128)(2,1)}, u32[]{:S(2)}, u32[]{:S(2)}) collective-permute-start(bf16[512,1024]{1,0:T(8,128)(2,1)} %slice.26), channel_id=1, source_target_pairs={{0,2},{2,4},{4,6},{6,7},{7,5},{5,3},{3,1},{1,0},{8,10},{10,12},{12... | collective-permute-start | bytes 3145736 | tf_op jit(solution)/shard_map/ppermute | solution.py:171
  316.2 36.5 %collective-permute-start.7 = (bf16[512,1024]{1,0:T(8,128)(2,1)}, bf16[512,1024]{1,0:T(8,128)(2,1)}, u32[]{:S(2)}, u32[]{:S(2)}) collective-permute-start(bf16[512,1024]{1,0:T(8,128)(2,1)} %slice.27), channel_id=1, source_target_pairs={{2,0},{4,2},{6,4},{7,6},{5,7},{3,5},{1,3},{0,1},{10,8},{12,10},{14... | collective-permute-start | bytes 3145736 | tf_op jit(solution)/shard_map/ppermute | solution.py:172
  318.2 32.0 %copy-start.3 = (bf16[12,128,1024]{2,1,0:T(8,128)(2,1)}, bf16[12,128,1024]{2,1,0:T(8,128)(2,1)S(1)}, u32[]{:S(2)}) copy-start(bf16[12,128,1024]{2,1,0:T(8,128)(2,1)S(1)} %all-to-all-done.6) | copy-start | bytes 9437188
  319.1 33.6 %all-to-all-start.4 = ((bf16[8,128,256]{2,1,0:T(8,128)(2,1)}), bf16[8,128,256]{2,1,0:T(8,128)(2,1)}, u32[]{:S(2)}, u32[]{:S(2)}) async-start(bf16[8,128,256]{2,1,0:T(8,128)(2,1)} %broadcast_in_dim.54), calls=%async_computation.4 | async-start | bytes 1048576 | tf_op jit(solution)/shard_map/all_to_all | solution.py:209
  352.7 20.4 %copy-start.1 = (s32[8]{0:T(128)S(1)}, s32[8]{0:T(128)}, u32[]{:S(2)}) copy-start(s32[8]{0:T(128)} %param.13) | copy-start | bytes 100

commit v3 on v2

--- a/solution.py
+++ b/solution.py
@@ -37,6 +37,7 @@
 def partial_kernel(count, with_acc, rows_ref, *refs):
     xs, ws = refs[:count], refs[count : 2 * count]
     out = refs[-1]
+    ws = [jnp.swapaxes(w[...], 0, 1) for w in ws]
     for h in range(2):
         total = refs[2 * count][h] if with_acc else None
         for x, w in zip(xs, ws):
@@ -53,7 +54,7 @@
     in_specs = [pl.BlockSpec((tokens, depth), lambda j, r: (0, 0))] * count
     for k in range(count):
         in_specs.append(
-            pl.BlockSpec((2, depth, block_cols), lambda j, r, k=k: (0, r[k], j))
+            pl.BlockSpec((depth, 2, block_cols), lambda j, r, k=k: (r[k], 0, j))
         )
     acc_spec = pl.BlockSpec((2, tokens, block_cols), lambda j, r: (0, 0, j))
     operands = list(xs) + [weight] * count
@@ -83,6 +84,7 @@
 
 def final_kernel(tiles_per_half, rank, rows_ref, seg_ref, xt, xb, w, acc, shrunk, b, out, total):
     narrow = out.shape[1]
+    w = jnp.swapaxes(w[...], 0, 1)
     for p, x in enumerate((xt, xb)):
         for h in range(2):
             span = slice(p * x.shape[0], (p + 1) * x.shape[0])
@@ -119,7 +121,7 @@
             in_specs=[
                 pl.BlockSpec((half, depth), lambda j, r, s: (0, 0)),
                 pl.BlockSpec((half, depth), lambda j, r, s: (0, 0)),
-                pl.BlockSpec((2, depth, narrow), lambda j, r, s: (0, r[0], j)),
+                pl.BlockSpec((depth, 2, narrow), lambda j, r, s: (r[0], 0, j)),
                 pl.BlockSpec((2, tokens, narrow), lambda j, r, s: (0, 0, j)),
                 pl.BlockSpec((tokens, 2 * rank), lambda j, r, s: (0, 0)),
                 pl.BlockSpec((1, segs, rank, twice), lambda j, r, s: (j, 0, 0, 0)),
@@ -214,7 +216,6 @@
         tiled=True,
     ).reshape(token_count, twice_rank)
 
-    weight = jnp.transpose(gate_up_weight, (1, 0, 2))
     acc = None
     for s in range(1, full_steps + 1):
         xs = [lefts[s], rights[s]]
@@ -222,9 +223,9 @@
         if s == 1:
             xs.insert(0, tokens)
             rows.insert(0, owner(0))
-        acc = partial_matmul(xs, weight, jnp.stack(rows), acc, block_cols)
+        acc = partial_matmul(xs, gate_up_weight, jnp.stack(rows), acc, block_cols)
     return final_matmul(
-        last_top, last_bottom, weight, jnp.stack([owner(n // 2)]), acc, shrunk, b, tile_seg
+        last_top, last_bottom, gate_up_weight, jnp.stack([owner(n // 2)]), acc, shrunk, b, tile_seg
     )
 
 

time: 374 us -> 378 us (1.011)
  local copies, waits for them, and re-layouts: 57.5 us -> 13.3 us
  waiting for transfers between devices: 115 us -> 155 us
  Pallas kernels: 107 us -> 112 us
    unnamed x15 -> x14, local copies, waits for them, and re-layouts: 44.3 us -> 0.03 us
    ppermute x3, waiting for transfers between devices: 77.3 us -> 107 us  [compute(): lefts.append(lax.ppermute(lefts[-1], TP, forward))]
    all_to_all x1, waiting for transfers between devices: 10.4 us -> 21.6 us  [compute(): lax.all_to_all(partial.reshape(n, share, twice_rank), TP, split_axis=0, c...]
  transfers between devices with their start and end apart: 13 -> 13, of which waited for: 4 -> 5; matrix products, arithmetic and copies ran while one was open for 17% -> 5% of each run, Pallas kernels for 23% -> 24%
where the time goes in v3:
time: 378 us; the launch traced here: 377 us
  waiting for transfers between devices  155 us (41%)
  Pallas kernels  112 us (30%)
  starting transfers between devices  46.3 us (12%)
  blocking collectives  41.8 us (11%)
  local copies, waits for them, and re-layouts  13.3 us (4%)
  other arithmetic  5.72 us (2%)
    ppermute x3, waiting for transfers between devices, compute(): lefts.append(lax.ppermute(lefts[-1], TP, forward))  107 us
    pallas_call x3, Pallas kernels, partial_matmul(): pl.pallas_call(functools.partial(partial_kernel, count, acc is not None),...  90.3 us
    all_to_all x1, waiting for transfers between devices, compute(): a = lax.all_to_all(a, TP, split_axis=0, concat_axis=0, tiled=True)  24.7 us
    all_to_all x1, blocking collectives, compute(): a = lax.all_to_all(a, 'grp', split_axis=0, concat_axis=0, tiled=True)  23.2 us
    pallas_call x1, Pallas kernels, final_matmul(): pl.pallas_call(functools.partial(final_kernel, half // TILE, rank), out_s...  21.9 us
    all_to_all x1, waiting for transfers between devices, compute(): lax.all_to_all(partial.reshape(n, share, twice_rank), TP, split_axis=0, c...  21.6 us
    ppermute x3, starting transfers between devices, compute(): lefts.append(lax.ppermute(lefts[-1], TP, forward))  20.1 us
    all_to_all x1, blocking collectives, compute(): a = lax.all_to_all(a, 'grp', split_axis=1, concat_axis=0, tiled=True)  18.6 us
  transfers between devices with their start and end apart: 13, of which 5 were waited for; matrix products, arithmetic and copies ran while one was open for 5% of the time, Pallas kernels for 24%

profile of v3, /device:TPU:0, one launch (start us, length us, event | category | flops | bytes accessed | tf_op | source)
XLA Modules:
  0.0 377.0 jit_solution(4480143271462419991)
XLA Ops:
  0.0 1.3 copy.15
  1.3 18.6 %all_to_all.45 = bf16[2,4,256,256]{3,2,0,1:T(8,128)(2,1)} all-to-all(bf16[2,4,256,256]{3,2,0,1:T(8,128)(2,1)S(1)} %copy.15), channel_id=1, replica_groups=mesh['grp'=4,'tp'=4,'cores'=2] {'grp'}, dimensions={1} | all-to-all | bytes 2097152 | tf_op jit(solution)/shard_map/all_to_all | solution.py:178
  19.9 6.3 %all-to-all-start.1 = ((bf16[8,256,256]{2,1,0:T(8,128)(2,1)}), bf16[8,256,256]{2,1,0:T(8,128)(2,1)S(1)}, u32[]{:S(2)}, u32[]{:S(2)}) async-start(bf16[8,256,256]{2,1,0:T(8,128)(2,1)} %bitcast.15), calls=%async_computation.1 | async-start | bytes 2097152 | tf_op jit(solution)/shard_map/all_to_all | solution.py:180
  27.1 24.7 %all-to-all-done.1 = bf16[8,256,256]{2,1,0:T(8,128)(2,1)S(1)} async-done(((bf16[8,256,256]{2,1,0:T(8,128)(2,1)}), bf16[8,256,256]{2,1,0:T(8,128)(2,1)S(1)}, u32[]{:S(2)}, u32[]{:S(2)}) %all-to-all-start.1) | async-done | bytes 1048608 | tf_op jit(solution)/shard_map/all_to_all | solution.py:180
  52.6 23.2 %all_to_all.46 = bf16[12,256,256]{2,1,0:T(8,128)(2,1)} all-to-all(bf16[12,256,256]{2,1,0:T(8,128)(2,1)S(1)} %broadcast_select_fusion.1), channel_id=1, replica_groups=mesh['grp'=4,'tp'=4,'cores'=2] {'grp'}, dimensions={0} | all-to-all | bytes 3145728 | tf_op jit(solution)/shard_map/all_to_all | solution.py:186
  75.9 4.5 %all-to-all-start.5 = ((bf16[8,128,1024]{2,1,0:T(8,128)(2,1)}), bf16[8,128,1024]{2,1,0:T(8,128)(2,1)}, u32[]{:S(2)}, u32[]{:S(2)}) async-start(bf16[8,128,1024]{2,1,0:T(8,128)(2,1)} %bitcast.49), calls=%async_computation.5 | async-start | bytes 4194304 | tf_op jit(solution)/shard_map/all_to_all | solution.py:182
  80.4 1.9 collective-permute-start
  82.8 77.3 %collective-permute-done.refs_1_ = bf16[1024,1024]{1,0:T(8,128)(2,1)} collective-permute-done((bf16[1024,1024]{1,0:T(8,128)(2,1)S(1)}, bf16[1024,1024]{1,0:T(8,128)(2,1)}, u32[]{:S(2)}, u32[]{:S(2)}) %collective-permute-start) | collective-permute-done | bytes 2097184 | tf_op jit(solution)/shard_map/ppermute | solution.py:171
  160.1 12.8 %collective-permute-start.1 = (bf16[1024,1024]{1,0:T(8,128)(2,1)}, bf16[1024,1024]{1,0:T(8,128)(2,1)}, u32[]{:S(2)}, u32[]{:S(2)}) collective-permute-start(bf16[1024,1024]{1,0:T(8,128)(2,1)} %collective-permute-done.refs_1_), channel_id=1, source_target_pairs={{0,2},{2,4},{4,6},{6,7},{7,5},{5,3},{3,1},{1,0},{8,10},{10,12},{12... | collective-permute-start | bytes 6291464 | tf_op jit(solution)/shard_map/ppermute | solution.py:171
  172.9 1.5 fusion.4
  174.3 0.8 fusion.5
  175.1 0.8 fusion.6
  175.9 0.8 fusion.1
  176.7 1.0 copy.22
  177.7 5.4 %all-to-all-start.3 = ((f32[8,128,256]{1,2,0:T(8,128)}), f32[8,128,256]{1,2,0:T(8,128)}, u32[]{:S(2)}, u32[]{:S(2)}) async-start(f32[8,128,256]{1,2,0:T(8,128)} %bitcast.46), calls=%async_computation.3 | async-start | bytes 2097152 | tf_op jit(solution)/shard_map/all_to_all | solution.py:207
  185.0 2.3 gather_fusion.2
  187.4 2.0 broadcast_select_fusion
  189.4 29.8 %collective-permute-done.1.refs_0_ = bf16[1024,1024]{1,0:T(8,128)(2,1)} collective-permute-done((bf16[1024,1024]{1,0:T(8,128)(2,1)}, bf16[1024,1024]{1,0:T(8,128)(2,1)}, u32[]{:S(2)}, u32[]{:S(2)}) %collective-permute-start.1) | collective-permute-done | bytes 2097184 | tf_op jit(solution)/shard_map/ppermute | solution.py:171
  219.2 5.4 %collective-permute-start.2 = (bf16[1024,1024]{1,0:T(8,128)(2,1)}, bf16[1024,1024]{1,0:T(8,128)(2,1)}, u32[]{:S(2)}, u32[]{:S(2)}) collective-permute-start(bf16[1024,1024]{1,0:T(8,128)(2,1)} %collective-permute-done.1.refs_0_), channel_id=1, source_target_pairs={{0,2},{2,4},{4,6},{6,7},{7,5},{5,3},{3,1},{1,0},{8,10},{10,12},{12... | collective-permute-start | bytes 6291464 | tf_op jit(solution)/shard_map/ppermute | solution.py:171
  224.6 21.6 %all-to-all-done.3 = f32[8,128,256]{1,2,0:T(8,128)} async-done(((f32[8,128,256]{1,2,0:T(8,128)}), f32[8,128,256]{1,2,0:T(8,128)}, u32[]{:S(2)}, u32[]{:S(2)}) %all-to-all-start.3) | async-done | bytes 1048608 | tf_op jit(solution)/shard_map/all_to_all | solution.py:207
  246.2 3.7 all-to-all-start.6
  249.9 35.0 %shard_map.73.refs_4_ = f32[2,1024,2048]{2,1,0:T(8,128)} custom-call(s32[3]{0:T(128)} %pad_add_fusion.2.rows_ref, bf16[1024,1024]{1,0:T(8,128)(2,1)} %refs_0_.1, bf16[1024,1024]{1,0:T(8,128)(2,1)} %collective-permute-done.refs_1_, bf16[1024,1024]{1,0:T(8,128)(2,1)} %collective-permute-done.4.refs_2_, bf16[8192,2,2048]{2,1,0:T(2,128)(2,1)} %w.1, ...), custom_call_target="tpu_custom_call" | custom-call | flops 25769803776 | bytes 58720256 | tf_op jit(solution)/shard_map/pallas_call | solution.py:66
  284.9 27.7 %shard_map.74.refs_4_ = f32[2,1024,2048]{2,1,0:T(8,128)} custom-call(s32[2]{0:T(128)} %pad_add_fusion.1.rows_ref, bf16[1024,1024]{1,0:T(8,128)(2,1)} %collective-permute-done.1.refs_0_, bf16[1024,1024]{1,0:T(8,128)(2,1)} %collective-permute-done.5.refs_1_, bf16[8192,2,2048]{2,1,0:T(2,128)(2,1)} %w.1, ...), custom_call_target="tpu_custom_call", output_to_operand_aliasing={{}: (5, {})} | custom-call | flops 17179869184 | bytes 50331648 | tf_op jit(solution)/shard_map/pallas_call | solution.py:66
  312.5 1.3 reduce_sum.19
  313.9 2.3 slice.26
  316.2 2.3 slice.27
  318.5 2.0 collective-permute-start.7
  320.6 0.9 broadcast_in_dim.54
  321.4 4.1 %all-to-all-start.4 = ((bf16[8,128,256]{2,1,0:T(8,128)(2,1)}), bf16[8,128,256]{2,1,0:T(8,128)(2,1)}, u32[]{:S(2)}, u32[]{:S(2)}) async-start(bf16[8,128,256]{2,1,0:T(8,128)(2,1)} %broadcast_in_dim.54), calls=%async_computation.4 | async-start | bytes 1048576 | tf_op jit(solution)/shard_map/all_to_all | solution.py:211
  325.6 27.7 %shard_map.75.acc = f32[2,1024,2048]{2,1,0:T(8,128)} custom-call(s32[2]{0:T(128)} %pad_add_fusion.rows_ref, bf16[1024,1024]{1,0:T(8,128)(2,1)} %collective-permute-done.2.refs_0_, bf16[1024,1024]{1,0:T(8,128)(2,1)} %collective-permute-done.6.refs_1_, bf16[8192,2,2048]{2,1,0:T(2,128)(2,1)} %w.1, ...), custom_call_target="tpu_custom_call", output_to_operand_aliasing={{}: (5, {})} | custom-call | flops 17179869184 | bytes 50331648 | tf_op jit(solution)/shard_map/pallas_call | solution.py:66
  353.3 1.8 all-to-all-done.4
  355.0 21.9 %shard_map.76 = bf16[1024,2048]{1,0:T(8,128)(2,1)} custom-call(s32[1]{0:T(128)} %bitcast.rows_ref, s32[8]{0:T(128)} %copy-done.5, bf16[512,1024]{1,0:T(8,128)(2,1)} %collective-permute-done.3.xt, bf16[512,1024]{1,0:T(8,128)(2,1)} %collective-permute-done.7.xb, bf16[8192,2,2048]{2,1,0:T(2,128)(2,1)} %w.1, f32[2,1024,2048]{2,1,0:T(8,128)} %shard_map.75.acc, ...), custom_call_target="tpu_custom_call" | custom-call | flops 9663676416 | bytes 29360128 | tf_op jit(solution)/shard_map/pallas_call | solution.py:115
  (44 shorter events, 4.3 us)
Async XLA Ops:
  0.0 26.4 %copy-start = (s32[8]{0:T(128)S(1)}, s32[8]{0:T(128)}, u32[]{:S(2)}) copy-start(s32[8]{0:T(128)} %param.13) | copy-start | bytes 100
  1.3 24.9 %copy-start.4 = (s32[4,3]{1,0:T(4,128)S(1)}, s32[4,3]{1,0:T(4,128)}, u32[]{:S(2)}) copy-start(s32[4,3]{1,0:T(4,128)} %param.11) | copy-start | bytes 148
  19.9 31.9 %all-to-all-start.1 = ((bf16[8,256,256]{2,1,0:T(8,128)(2,1)}), bf16[8,256,256]{2,1,0:T(8,128)(2,1)S(1)}, u32[]{:S(2)}, u32[]{:S(2)}) async-start(bf16[8,256,256]{2,1,0:T(8,128)(2,1)} %bitcast.15), calls=%async_computation.1 | async-start | bytes 2097152 | tf_op jit(solution)/shard_map/all_to_all | solution.py:180
  75.9 4.5 %copy-start.2 = (bf16[1024,1024]{1,0:T(8,128)(2,1)S(1)}, bf16[1024,1024]{1,0:T(8,128)(2,1)}, u32[]{:S(2)}) copy-start(bf16[1024,1024]{1,0:T(8,128)(2,1)} %refs_0_.1) | copy-start | bytes 6291460
  75.9 6.6 %copy-start.6 = (s32[1,3]{1,0:T(1,128)S(1)}, s32[1,3]{1,0:T(1,128)}, u32[]{:S(2)}) copy-start(s32[1,3]{1,0:T(1,128)} %param.12) | copy-start | bytes 40
  75.9 101.9 %all-to-all-start.5 = ((bf16[8,128,1024]{2,1,0:T(8,128)(2,1)}), bf16[8,128,1024]{2,1,0:T(8,128)(2,1)}, u32[]{:S(2)}, u32[]{:S(2)}) async-start(bf16[8,128,1024]{2,1,0:T(8,128)(2,1)} %bitcast.49), calls=%async_computation.5 | async-start | bytes 4194304 | tf_op jit(solution)/shard_map/all_to_all | solution.py:182
  80.4 79.7 %collective-permute-start = (bf16[1024,1024]{1,0:T(8,128)(2,1)S(1)}, bf16[1024,1024]{1,0:T(8,128)(2,1)}, u32[]{:S(2)}, u32[]{:S(2)}) collective-permute-start(bf16[1024,1024]{1,0:T(8,128)(2,1)S(1)} %copy-done.2), channel_id=1, source_target_pairs={{0,2},{2,4},{4,6},{6,7},{7,5},{5,3},{3,1},{1,0},{8,10},{10,12},{12... | collective-permute-start | bytes 6291464 | tf_op jit(solution)/shard_map/ppermute | solution.py:171
  82.3 90.6 %collective-permute-start.4 = (bf16[1024,1024]{1,0:T(8,128)(2,1)S(1)}, bf16[1024,1024]{1,0:T(8,128)(2,1)}, u32[]{:S(2)}, u32[]{:S(2)}) collective-permute-start(bf16[1024,1024]{1,0:T(8,128)(2,1)S(1)} %copy-done.2), channel_id=1, source_target_pairs={{2,0},{4,2},{6,4},{7,6},{5,7},{3,5},{1,3},{0,1},{10,8},{12,10},{14... | collective-permute-start | bytes 6291464 | tf_op jit(solution)/shard_map/ppermute | solution.py:172
  82.7 92.4 %copy-start.5 = (s32[8]{0:T(128)}, s32[8]{0:T(128)S(1)}, u32[]{:S(2)}) copy-start(s32[8]{0:T(128)S(1)} %convert_reduce_fusion.seg_ref) | copy-start | bytes 100
  160.1 59.1 %collective-permute-start.1 = (bf16[1024,1024]{1,0:T(8,128)(2,1)}, bf16[1024,1024]{1,0:T(8,128)(2,1)}, u32[]{:S(2)}, u32[]{:S(2)}) collective-permute-start(bf16[1024,1024]{1,0:T(8,128)(2,1)} %collective-permute-done.refs_1_), channel_id=1, source_target_pairs={{0,2},{2,4},{4,6},{6,7},{7,5},{5,3},{3,1},{1,0},{8,10},{10,12},{12... | collective-permute-start | bytes 6291464 | tf_op jit(solution)/shard_map/ppermute | solution.py:171
  172.9 51.7 %collective-permute-start.5 = (bf16[1024,1024]{1,0:T(8,128)(2,1)}, bf16[1024,1024]{1,0:T(8,128)(2,1)}, u32[]{:S(2)}, u32[]{:S(2)}) collective-permute-start(bf16[1024,1024]{1,0:T(8,128)(2,1)} %collective-permute-done.4.refs_2_), channel_id=1, source_target_pairs={{2,0},{4,2},{6,4},{7,6},{5,7},{3,5},{1,3},{0,1},{10,8},{12,10},{14... | collective-permute-start | bytes 6291464 | tf_op jit(solution)/shard_map/ppermute | solution.py:172
  177.7 68.5 %all-to-all-start.3 = ((f32[8,128,256]{1,2,0:T(8,128)}), f32[8,128,256]{1,2,0:T(8,128)}, u32[]{:S(2)}, u32[]{:S(2)}) async-start(f32[8,128,256]{1,2,0:T(8,128)} %bitcast.46), calls=%async_computation.3 | async-start | bytes 2097152 | tf_op jit(solution)/shard_map/all_to_all | solution.py:207
  219.2 94.7 %collective-permute-start.2 = (bf16[1024,1024]{1,0:T(8,128)(2,1)}, bf16[1024,1024]{1,0:T(8,128)(2,1)}, u32[]{:S(2)}, u32[]{:S(2)}) collective-permute-start(bf16[1024,1024]{1,0:T(8,128)(2,1)} %collective-permute-done.1.refs_0_), channel_id=1, source_target_pairs={{0,2},{2,4},{4,6},{6,7},{7,5},{5,3},{3,1},{1,0},{8,10},{10,12},{12... | collective-permute-start | bytes 6291464 | tf_op jit(solution)/shard_map/ppermute | solution.py:171
  224.6 91.7 %collective-permute-start.6 = (bf16[1024,1024]{1,0:T(8,128)(2,1)}, bf16[1024,1024]{1,0:T(8,128)(2,1)}, u32[]{:S(2)}, u32[]{:S(2)}) collective-permute-start(bf16[1024,1024]{1,0:T(8,128)(2,1)} %collective-permute-done.5.refs_1_), channel_id=1, source_target_pairs={{2,0},{4,2},{6,4},{7,6},{5,7},{3,5},{1,3},{0,1},{10,8},{12,10},{14... | collective-permute-start | bytes 6291464 | tf_op jit(solution)/shard_map/ppermute | solution.py:172
  246.2 74.3 %all-to-all-start.6 = ((bf16[12,128,1024]{2,1,0:T(8,128)(2,1)}), bf16[12,128,1024]{2,1,0:T(8,128)(2,1)S(1)}, u32[]{:S(2)}, u32[]{:S(2)}) async-start(bf16[12,128,1024]{2,1,0:T(8,128)(2,1)} %broadcast_select_fusion), calls=%async_computation.6 | async-start | bytes 6291456 | tf_op jit(solution)/shard_map/all_to_all | solution.py:187
  316.2 38.8 %collective-permute-start.3 = (bf16[512,1024]{1,0:T(8,128)(2,1)}, bf16[512,1024]{1,0:T(8,128)(2,1)}, u32[]{:S(2)}, u32[]{:S(2)}) collective-permute-start(bf16[512,1024]{1,0:T(8,128)(2,1)} %slice.26), channel_id=1, source_target_pairs={{0,2},{2,4},{4,6},{6,7},{7,5},{5,3},{3,1},{1,0},{8,10},{10,12},{12... | collective-permute-start | bytes 3145736 | tf_op jit(solution)/shard_map/ppermute | solution.py:173
  318.5 36.5 %collective-permute-start.7 = (bf16[512,1024]{1,0:T(8,128)(2,1)}, bf16[512,1024]{1,0:T(8,128)(2,1)}, u32[]{:S(2)}, u32[]{:S(2)}) collective-permute-start(bf16[512,1024]{1,0:T(8,128)(2,1)} %slice.27), channel_id=1, source_target_pairs={{2,0},{4,2},{6,4},{7,6},{5,7},{3,5},{1,3},{0,1},{10,8},{12,10},{14... | collective-permute-start | bytes 3145736 | tf_op jit(solution)/shard_map/ppermute | solution.py:174
  320.6 32.7 %copy-start.3 = (bf16[12,128,1024]{2,1,0:T(8,128)(2,1)}, bf16[12,128,1024]{2,1,0:T(8,128)(2,1)S(1)}, u32[]{:S(2)}) copy-start(bf16[12,128,1024]{2,1,0:T(8,128)(2,1)S(1)} %all-to-all-done.6) | copy-start | bytes 9437188
  321.4 33.6 %all-to-all-start.4 = ((bf16[8,128,256]{2,1,0:T(8,128)(2,1)}), bf16[8,128,256]{2,1,0:T(8,128)(2,1)}, u32[]{:S(2)}, u32[]{:S(2)}) async-start(bf16[8,128,256]{2,1,0:T(8,128)(2,1)} %broadcast_in_dim.54), calls=%async_computation.4 | async-start | bytes 1048576 | tf_op jit(solution)/shard_map/all_to_all | solution.py:211
  355.0 21.9 %copy-start.1 = (s32[8]{0:T(128)S(1)}, s32[8]{0:T(128)}, u32[]{:S(2)}) copy-start(s32[8]{0:T(128)} %param.13) | copy-start | bytes 100

commit v4 on v3

--- a/solution.py
+++ b/solution.py
@@ -12,6 +12,7 @@
 VMEM_LIMIT = 60 * 1024 * 1024
 
 adapter_scale = 0.5
+
 
 TP = ("tp", "cores")
 
@@ -138,6 +139,21 @@
     )(rows, tile_seg, xt, xb, weight, acc, shrunk, b_chosen)
 
 
+def group_exchange(pool, slots):
+    groups = lax.axis_size("grp")
+    g = lax.axis_index("grp")
+    parts = []
+    for k in range(groups):
+        wanted = lax.dynamic_index_in_dim(slots, (g + k) % groups, 0, keepdims=False)
+        part = jnp.take(pool, wanted, axis=0, mode="clip")
+        if k:
+            pairs = [(i, (i + k) % groups) for i in range(groups)]
+            part = lax.ppermute(part, "grp", pairs)
+        parts.append(part)
+    sources = (g + groups - jnp.arange(groups)) % groups
+    return jnp.take(jnp.stack(parts), sources, axis=0, mode="clip")
+
+
 def compute(
     tokens,
     gate_up_weight,
@@ -180,13 +196,9 @@
     a = lax.all_to_all(a, TP, split_axis=0, concat_axis=0, tiled=True)
     b = up_factor_pool.reshape(up_factor_pool.shape[2:])
     b = lax.all_to_all(b, TP, split_axis=0, concat_axis=0, tiled=True)
-    slots = jnp.take(adapter_pool_rows, segment_adapters.reshape(-1))
-    a = jnp.take(a, slots, axis=0)
-    b = jnp.take(b, slots, axis=0)
-    a = lax.all_to_all(a, "grp", split_axis=0, concat_axis=0, tiled=True)
-    b = lax.all_to_all(b, "grp", split_axis=0, concat_axis=0, tiled=True)
-    a = a.reshape(groups, seg_count, piece, twice_rank)
-    b = b.reshape(groups, seg_count, *b.shape[1:])
+    slots = jnp.take(adapter_pool_rows, segment_adapters, mode="clip")
+    a = group_exchange(a, slots)
+    b = group_exchange(b, slots)
     block_cols = narrow
     if narrow % 128:
         block_cols = local_hidden_width

time: 378 us -> 302 us (0.80)
  waiting for transfers between devices: 155 us -> 107 us
  blocking collectives: 41.8 us -> 0 us
  local copies, waits for them, and re-layouts: 13.3 us -> 31.8 us
  starting transfers between devices: 46.3 us -> 39.3 us
    ppermute x3, waiting for transfers between devices: 107 us -> 22.4 us  [compute(): lefts.append(lax.ppermute(lefts[-1], TP, forward))]
    all_to_all x2 -> x0, blocking collectives: 41.8 us -> none  [the longest x1 23.2 us: compute(): a = lax.all_to_all(a, 'grp', split_axis=0, concat_axis=0, tiled=True)]
    all_to_all x1, waiting for transfers between devices: 0.01 us -> 29.9 us  [compute(): b = lax.all_to_all(b, TP, split_axis=0, concat_axis=0, tiled=True)]
    gather x3 -> x12, local copies, waits for them, and re-layouts: 3.64 us -> 17.4 us  [the longest x8 10.8 us: group_exchange(): part = jnp.take(pool, wanted, axis=0, mode='clip')]
    ppermute x3, starting transfers between devices: 20.1 us -> 7.83 us  [compute(): lefts.append(lax.ppermute(lefts[-1], TP, forward))]
    all_to_all x1, waiting for transfers between devices: 0.01 us -> 12 us  [compute(): a = lax.all_to_all(a, 'grp', split_axis=1, concat_axis=0, tiled=True)]
    ppermute x0 -> x6, starting transfers between devices: none -> 6.78 us  [group_exchange(): part = lax.ppermute(part, 'grp', pairs)]
    another operation x1 -> x3, other arithmetic: 0.18 us -> 4.56 us  [the longest x2 4.39 us: group_exchange(): return jnp.take(jnp.stack(parts), sources, axis=0, mode='clip')]
  transfers between devices with their start and end apart: 13 -> 19, of which waited for: 5 -> 6; matrix products, arithmetic and copies ran while one was open for 5% -> 12% of each run, Pallas kernels for 24% -> 30%
where the time goes in v4:
time: 302 us; the launch traced here: 301 us
  Pallas kernels  112 us (37%)
  waiting for transfers between devices  107 us (35%)
  starting transfers between devices  39.3 us (13%)
  local copies, waits for them, and re-layouts  31.8 us (11%)
  other arithmetic  8.5 us (3%)
    pallas_call x3, Pallas kernels, partial_matmul(): pl.pallas_call(functools.partial(partial_kernel, count, acc is not None),...  90.4 us
    all_to_all x1, waiting for transfers between devices, compute(): b = lax.all_to_all(b, TP, split_axis=0, concat_axis=0, tiled=True)  29.9 us
    ppermute x3, waiting for transfers between devices, compute(): lefts.append(lax.ppermute(lefts[-1], TP, forward))  22.4 us
    all_to_all x1, waiting for transfers between devices, compute(): a = lax.all_to_all(a, TP, split_axis=0, concat_axis=0, tiled=True)  22 us
    pallas_call x1, Pallas kernels, final_matmul(): pl.pallas_call(functools.partial(final_kernel, half // TILE, rank), out_s...  21.9 us
    all_to_all x1, waiting for transfers between devices, compute(): lax.all_to_all(partial.reshape(n, share, twice_rank), TP, split_axis=0, c...  19.8 us
    all_to_all x1, waiting for transfers between devices, compute(): a = lax.all_to_all(a, 'grp', split_axis=1, concat_axis=0, tiled=True)  12 us
    gather x8, local copies, waits for them, and re-layouts, group_exchange(): part = jnp.take(pool, wanted, axis=0, mode='clip')  10.8 us
  transfers between devices with their start and end apart: 19, of which 6 were waited for; matrix products, arithmetic and copies ran while one was open for 12% of the time, Pallas kernels for 30%

profile of v4, /device:TPU:0, one launch (start us, length us, event | category | flops | bytes accessed | tf_op | source)
XLA Modules:
  0.0 301.3 jit_solution(11570532062872448000)
XLA Ops:
  0.0 2.4 copy.15
  2.4 4.4 %all-to-all-start = ((bf16[2,4,256,256]{3,2,0,1:T(8,128)(2,1)}), bf16[2,4,256,256]{3,2,0,1:T(8,128)(2,1)S(1)}, u32[]{:S(2)}, u32[]{:S(2)}) async-start(bf16[2,4,256,256]{3,2,0,1:T(8,128)(2,1)} %copy.15), calls=%async_computation | async-start | bytes 2097152 | tf_op jit(solution)/shard_map/all_to_all | solution.py:194
  6.8 2.4 collective-permute-start
  9.2 12.0 %all-to-all-done = bf16[2,4,256,256]{3,2,0,1:T(8,128)(2,1)S(1)} async-done(((bf16[2,4,256,256]{3,2,0,1:T(8,128)(2,1)}), bf16[2,4,256,256]{3,2,0,1:T(8,128)(2,1)S(1)}, u32[]{:S(2)}, u32[]{:S(2)}) %all-to-all-start) | async-done | bytes 1048608 | tf_op jit(solution)/shard_map/all_to_all | solution.py:194
  22.2 6.7 %all-to-all-start.1 = ((bf16[8,256,256]{2,1,0:T(8,128)(2,1)}), bf16[8,256,256]{2,1,0:T(8,128)(2,1)S(1)}, u32[]{:S(2)}, u32[]{:S(2)}) async-start(bf16[8,256,256]{2,1,0:T(8,128)(2,1)} %bitcast.55), calls=%async_computation.1 | async-start | bytes 2097152 | tf_op jit(solution)/shard_map/all_to_all | solution.py:196
  33.3 22.4 %collective-permute-done.refs_1_ = bf16[1024,1024]{1,0:T(8,128)(2,1)} collective-permute-done((bf16[1024,1024]{1,0:T(8,128)(2,1)S(1)}, bf16[1024,1024]{1,0:T(8,128)(2,1)}, u32[]{:S(2)}, u32[]{:S(2)}) %collective-permute-start) | collective-permute-done | bytes 2097184 | tf_op jit(solution)/shard_map/ppermute | solution.py:187
  55.7 3.4 %collective-permute-start.1 = (bf16[1024,1024]{1,0:T(8,128)(2,1)}, bf16[1024,1024]{1,0:T(8,128)(2,1)}, u32[]{:S(2)}, u32[]{:S(2)}) collective-permute-start(bf16[1024,1024]{1,0:T(8,128)(2,1)} %collective-permute-done.refs_1_), channel_id=1, source_target_pairs={{0,2},{2,4},{4,6},{6,7},{7,5},{5,3},{3,1},{1,0},{8,10},{10,12},{12... | collective-permute-start | bytes 6291464 | tf_op jit(solution)/shard_map/ppermute | solution.py:187
  59.2 22.0 %all-to-all-done.1 = bf16[8,256,256]{2,1,0:T(8,128)(2,1)S(1)} async-done(((bf16[8,256,256]{2,1,0:T(8,128)(2,1)}), bf16[8,256,256]{2,1,0:T(8,128)(2,1)S(1)}, u32[]{:S(2)}, u32[]{:S(2)}) %all-to-all-start.1) | async-done | bytes 1048608 | tf_op jit(solution)/shard_map/all_to_all | solution.py:196
  81.2 3.6 %all-to-all-start.4 = ((bf16[8,128,1024]{2,1,0:T(8,128)(2,1)}), bf16[8,128,1024]{2,1,0:T(8,128)(2,1)S(1)}, u32[]{:S(2)}, u32[]{:S(2)}) async-start(bf16[8,128,1024]{2,1,0:T(8,128)(2,1)} %bitcast.58), calls=%async_computation.4 | async-start | bytes 4194304 | tf_op jit(solution)/shard_map/all_to_all | solution.py:198
  87.5 1.9 collective-permute-start.9
  92.3 34.9 %shard_map.73.refs_4_ = f32[2,1024,2048]{2,1,0:T(8,128)} custom-call(s32[3]{0:T(128)} %pad_add_fusion.2.rows_ref, bf16[1024,1024]{1,0:T(8,128)(2,1)} %refs_0_.1, bf16[1024,1024]{1,0:T(8,128)(2,1)} %collective-permute-done.refs_1_, bf16[1024,1024]{1,0:T(8,128)(2,1)} %collective-permute-done.4.refs_2_, bf16[8192,2,2048]{2,1,0:T(2,128)(2,1)} %w.1, ...), custom_call_target="tpu_custom_call" | custom-call | flops 25769803776 | bytes 58720256 | tf_op jit(solution)/shard_map/pallas_call | solution.py:67
  127.8 2.6 pad_maximum_fusion.1
  130.4 3.3 %gather_fusion.5 = bf16[4,3,256,256]{3,2,1,0:T(8,128)(2,1)} fusion(bf16[4,3,256,256]{3,2,1,0:T(8,128)(2,1)} %pad_maximum_fusion.1, s32[1024]{0:T(1024)} %pad_clamp_fusion), kind=kCustom, calls=%fused_computation.5 | custom fusion | bytes 3145744 | tf_op jit(solution)/shard_map/jit(_take)/gather | solution.py:154
  133.7 1.6 fusion.8
  137.3 2.0 collective-permute-start.2
  141.3 29.9 %all-to-all-done.4 = bf16[8,128,1024]{2,1,0:T(8,128)(2,1)S(1)} async-done(((bf16[8,128,1024]{2,1,0:T(8,128)(2,1)}), bf16[8,128,1024]{2,1,0:T(8,128)(2,1)S(1)}, u32[]{:S(2)}, u32[]{:S(2)}) %all-to-all-start.4) | async-done | bytes 2097184 | tf_op jit(solution)/shard_map/all_to_all | solution.py:198
  171.2 4.3 %all-to-all-start.2 = ((f32[8,128,256]{1,2,0:T(8,128)}), f32[8,128,256]{1,2,0:T(8,128)}, u32[]{:S(2)}, u32[]{:S(2)}) async-start(f32[8,128,256]{1,2,0:T(8,128)} %bitcast.54), calls=%async_computation.2 | async-start | bytes 2097152 | tf_op jit(solution)/shard_map/all_to_all | solution.py:219
  175.4 1.6 gather_fusion.7
  177.0 1.5 gather_fusion.8
  178.6 1.9 collective-permute-start.12
  180.5 1.5 gather_fusion.9
  183.5 1.5 gather_fusion.6
  185.0 27.8 %shard_map.74.refs_4_ = f32[2,1024,2048]{2,1,0:T(8,128)} custom-call(s32[2]{0:T(128)} %pad_add_fusion.1.rows_ref, bf16[1024,1024]{1,0:T(8,128)(2,1)} %collective-permute-done.1.refs_0_, bf16[1024,1024]{1,0:T(8,128)(2,1)} %collective-permute-done.5.refs_1_, bf16[8192,2,2048]{2,1,0:T(2,128)(2,1)} %w.1, ...), custom_call_target="tpu_custom_call", output_to_operand_aliasing={{}: (5, {})} | custom-call | flops 17179869184 | bytes 50331648 | tf_op jit(solution)/shard_map/pallas_call | solution.py:67
  213.7 1.8 pad_maximum_fusion
  215.5 2.5 gather_fusion.10
  218.0 19.8 %all-to-all-done.2 = f32[8,128,256]{1,2,0:T(8,128)} async-done(((f32[8,128,256]{1,2,0:T(8,128)}), f32[8,128,256]{1,2,0:T(8,128)}, u32[]{:S(2)}, u32[]{:S(2)}) %all-to-all-start.2) | async-done | bytes 1048608 | tf_op jit(solution)/shard_map/all_to_all | solution.py:219
  240.1 3.6 %all-to-all-start.3 = ((bf16[8,128,256]{2,1,0:T(8,128)(2,1)}), bf16[8,128,256]{2,1,0:T(8,128)(2,1)S(1)}, u32[]{:S(2)}, u32[]{:S(2)}) async-start(bf16[8,128,256]{2,1,0:T(8,128)(2,1)} %broadcast_in_dim.61), calls=%async_computation.3 | async-start | bytes 1048576 | tf_op jit(solution)/shard_map/all_to_all | solution.py:223
  243.7 2.3 slice.42
  245.9 2.0 collective-permute-start.3
  248.0 2.3 slice.43
  250.2 27.7 %shard_map.75.acc = f32[2,1024,2048]{2,1,0:T(8,128)} custom-call(s32[2]{0:T(128)} %pad_add_fusion.rows_ref, bf16[1024,1024]{1,0:T(8,128)(2,1)} %collective-permute-done.2.refs_0_, bf16[1024,1024]{1,0:T(8,128)(2,1)} %collective-permute-done.6.refs_1_, bf16[8192,2,2048]{2,1,0:T(2,128)(2,1)} %w.1, ...), custom_call_target="tpu_custom_call", output_to_operand_aliasing={{}: (5, {})} | custom-call | flops 17179869184 | bytes 50331648 | tf_op jit(solution)/shard_map/pallas_call | solution.py:67
  279.4 21.9 %shard_map.76 = bf16[1024,2048]{1,0:T(8,128)(2,1)} custom-call(s32[1]{0:T(128)} %bitcast.rows_ref, s32[8]{0:T(128)} %copy-done.14, bf16[512,1024]{1,0:T(8,128)(2,1)} %copy-done.7, bf16[512,1024]{1,0:T(8,128)(2,1)} %copy-done.8, bf16[8192,2,2048]{2,1,0:T(2,128)(2,1)} %w.1, f32[2,1024,2048]{2,1,0:T(8,128)} %shard_map.75.acc, bf16[1024,256]{1,0:T(8,128)(2,1)} %bitcast.57, ...), custom_call_target="tpu_custom_call" | custom-call | flops 9663676416 | bytes 29360128 | tf_op jit(solution)/shard_map/pallas_call | solution.py:116
  (83 shorter events, 21.4 us)
Async XLA Ops:
  0.0 29.0 %copy-start = (s32[8]{0:T(128)S(1)}, s32[8]{0:T(128)}, u32[]{:S(2)}) copy-start(s32[8]{0:T(128)} %param.13) | copy-start | bytes 100
  0.0 6.8 %copy-start.2 = (bf16[1024,1024]{1,0:T(8,128)(2,1)S(1)}, bf16[1024,1024]{1,0:T(8,128)(2,1)}, u32[]{:S(2)}) copy-start(bf16[1024,1024]{1,0:T(8,128)(2,1)} %refs_0_.1) | copy-start | bytes 6291460
  2.4 26.5 %copy-start.13 = (s32[4,3]{1,0:T(4,128)S(1)}, s32[4,3]{1,0:T(4,128)}, u32[]{:S(2)}) copy-start(s32[4,3]{1,0:T(4,128)} %param.11) | copy-start | bytes 148
  2.4 18.8 %all-to-all-start = ((bf16[2,4,256,256]{3,2,0,1:T(8,128)(2,1)}), bf16[2,4,256,256]{3,2,0,1:T(8,128)(2,1)S(1)}, u32[]{:S(2)}, u32[]{:S(2)}) async-start(bf16[2,4,256,256]{3,2,0,1:T(8,128)(2,1)} %copy.15), calls=%async_computation | async-start | bytes 2097152 | tf_op jit(solution)/shard_map/all_to_all | solution.py:194
  6.8 48.9 %collective-permute-start = (bf16[1024,1024]{1,0:T(8,128)(2,1)S(1)}, bf16[1024,1024]{1,0:T(8,128)(2,1)}, u32[]{:S(2)}, u32[]{:S(2)}) collective-permute-start(bf16[1024,1024]{1,0:T(8,128)(2,1)S(1)} %copy-done.2), channel_id=1, source_target_pairs={{0,2},{2,4},{4,6},{6,7},{7,5},{5,3},{3,1},{1,0},{8,10},{10,12},{12... | collective-permute-start | bytes 6291464 | tf_op jit(solution)/shard_map/ppermute | solution.py:187
  9.2 50.0 %collective-permute-start.4 = (bf16[1024,1024]{1,0:T(8,128)(2,1)S(1)}, bf16[1024,1024]{1,0:T(8,128)(2,1)}, u32[]{:S(2)}, u32[]{:S(2)}) collective-permute-start(bf16[1024,1024]{1,0:T(8,128)(2,1)S(1)} %copy-done.2), channel_id=1, source_target_pairs={{2,0},{4,2},{6,4},{7,6},{5,7},{3,5},{1,3},{0,1},{10,8},{12,10},{14... | collective-permute-start | bytes 6291464 | tf_op jit(solution)/shard_map/ppermute | solution.py:188
  22.2 7.5 %copy-start.15 = (s32[1,3]{1,0:T(1,128)S(1)}, s32[1,3]{1,0:T(1,128)}, u32[]{:S(2)}) copy-start(s32[1,3]{1,0:T(1,128)} %param.12) | copy-start | bytes 40
  22.2 59.0 %all-to-all-start.1 = ((bf16[8,256,256]{2,1,0:T(8,128)(2,1)}), bf16[8,256,256]{2,1,0:T(8,128)(2,1)S(1)}, u32[]{:S(2)}, u32[]{:S(2)}) async-start(bf16[8,256,256]{2,1,0:T(8,128)(2,1)} %bitcast.55), calls=%async_computation.1 | async-start | bytes 2097152 | tf_op jit(solution)/shard_map/all_to_all | solution.py:196
  31.9 53.0 %copy-start.10 = (s32[1024]{0:T(1024)}, s32[1024]{0:T(1024)S(1)}, u32[]{:S(2)}) copy-start(s32[1024]{0:T(1024)S(1)} %pad_clamp_fusion.3) | copy-start | bytes 12292
  32.6 26.6 %copy-start.14 = (s32[8]{0:T(128)}, s32[8]{0:T(128)S(1)}, u32[]{:S(2)}) copy-start(s32[8]{0:T(128)S(1)} %convert_reduce_fusion.seg_ref) | copy-start | bytes 100
  55.7 81.6 %collective-permute-start.1 = (bf16[1024,1024]{1,0:T(8,128)(2,1)}, bf16[1024,1024]{1,0:T(8,128)(2,1)}, u32[]{:S(2)}, u32[]{:S(2)}) collective-permute-start(bf16[1024,1024]{1,0:T(8,128)(2,1)} %collective-permute-done.refs_1_), channel_id=1, source_target_pairs={{0,2},{2,4},{4,6},{6,7},{7,5},{5,3},{3,1},{1,0},{8,10},{10,12},{12... | collective-permute-start | bytes 6291464 | tf_op jit(solution)/shard_map/ppermute | solution.py:187
  59.2 80.2 %collective-permute-start.5 = (bf16[1024,1024]{1,0:T(8,128)(2,1)}, bf16[1024,1024]{1,0:T(8,128)(2,1)}, u32[]{:S(2)}, u32[]{:S(2)}) collective-permute-start(bf16[1024,1024]{1,0:T(8,128)(2,1)} %collective-permute-done.4.refs_2_), channel_id=1, source_target_pairs={{2,0},{4,2},{6,4},{7,6},{5,7},{3,5},{1,3},{0,1},{10,8},{12,10},{14... | collective-permute-start | bytes 6291464 | tf_op jit(solution)/shard_map/ppermute | solution.py:188
  81.2 89.9 %all-to-all-start.4 = ((bf16[8,128,1024]{2,1,0:T(8,128)(2,1)}), bf16[8,128,1024]{2,1,0:T(8,128)(2,1)S(1)}, u32[]{:S(2)}, u32[]{:S(2)}) async-start(bf16[8,128,1024]{2,1,0:T(8,128)(2,1)} %bitcast.58), calls=%async_computation.4 | async-start | bytes 4194304 | tf_op jit(solution)/shard_map/all_to_all | solution.py:198
  86.2 41.6 %collective-permute-start.8 = (bf16[3,256,256]{2,1,0:T(8,128)(2,1)}, bf16[3,256,256]{2,1,0:T(8,128)(2,1)}, u32[]{:S(2)}, u32[]{:S(2)}) collective-permute-start(bf16[3,256,256]{2,1,0:T(8,128)(2,1)} %gather_fusion.2), channel_id=1, source_target_pairs={{0,8},{8,16},{16,24},{24,0},{1,9},{9,17},{17,25},{25,1},{2,10},{10... | collective-permute-start | bytes 1179656 | tf_op jit(solution)/shard_map/ppermute | solution.py:151
  87.5 40.2 %collective-permute-start.9 = (bf16[3,256,256]{2,1,0:T(8,128)(2,1)}, bf16[3,256,256]{2,1,0:T(8,128)(2,1)}, u32[]{:S(2)}, u32[]{:S(2)}) collective-permute-start(bf16[3,256,256]{2,1,0:T(8,128)(2,1)} %gather_fusion.3), channel_id=1, source_target_pairs={{0,16},{8,24},{16,0},{24,8},{1,17},{9,25},{17,1},{25,9},{2,18},{10... | collective-permute-start | bytes 1179656 | tf_op jit(solution)/shard_map/ppermute | solution.py:151
  90.8 37.0 %collective-permute-start.10 = (bf16[3,256,256]{2,1,0:T(8,128)(2,1)}, bf16[3,256,256]{2,1,0:T(8,128)(2,1)}, u32[]{:S(2)}, u32[]{:S(2)}) collective-permute-start(bf16[3,256,256]{2,1,0:T(8,128)(2,1)} %gather_fusion.4), channel_id=1, source_target_pairs={{0,24},{8,0},{16,8},{24,16},{1,25},{9,1},{17,9},{25,17},{2,26},{10... | collective-permute-start | bytes 1179656 | tf_op jit(solution)/shard_map/ppermute | solution.py:151
  133.7 2.1 copy-start.3
  136.5 2.9 copy-start.11
  136.5 2.9 copy-start.12
  137.3 106.3 %collective-permute-start.2 = (bf16[1024,1024]{1,0:T(8,128)(2,1)}, bf16[1024,1024]{1,0:T(8,128)(2,1)}, u32[]{:S(2)}, u32[]{:S(2)}) collective-permute-start(bf16[1024,1024]{1,0:T(8,128)(2,1)} %collective-permute-done.1.refs_0_), channel_id=1, source_target_pairs={{0,2},{2,4},{4,6},{6,7},{7,5},{5,3},{3,1},{1,0},{8,10},{10,12},{12... | collective-permute-start | bytes 6291464 | tf_op jit(solution)/shard_map/ppermute | solution.py:187
  139.3 108.6 %collective-permute-start.6 = (bf16[1024,1024]{1,0:T(8,128)(2,1)}, bf16[1024,1024]{1,0:T(8,128)(2,1)}, u32[]{:S(2)}, u32[]{:S(2)}) collective-permute-start(bf16[1024,1024]{1,0:T(8,128)(2,1)} %collective-permute-done.5.refs_1_), channel_id=1, source_target_pairs={{2,0},{4,2},{6,4},{7,6},{5,7},{3,5},{1,3},{0,1},{10,8},{12,10},{14... | collective-permute-start | bytes 6291464 | tf_op jit(solution)/shard_map/ppermute | solution.py:188
  171.2 66.7 %all-to-all-start.2 = ((f32[8,128,256]{1,2,0:T(8,128)}), f32[8,128,256]{1,2,0:T(8,128)}, u32[]{:S(2)}, u32[]{:S(2)}) async-start(f32[8,128,256]{1,2,0:T(8,128)} %bitcast.54), calls=%async_computation.2 | async-start | bytes 2097152 | tf_op jit(solution)/shard_map/all_to_all | solution.py:219
  177.0 35.8 %collective-permute-start.11 = (bf16[3,128,1024]{2,1,0:T(8,128)(2,1)}, bf16[3,128,1024]{2,1,0:T(8,128)(2,1)S(1)}, u32[]{:S(2)}, u32[]{:S(2)}) collective-permute-start(bf16[3,128,1024]{2,1,0:T(8,128)(2,1)} %gather_fusion.7), channel_id=1, source_target_pairs={{0,8},{8,16},{16,24},{24,0},{1,9},{9,17},{17,25},{25,1},{2,10},{10... | collective-permute-start | bytes 2359304 | tf_op jit(solution)/shard_map/ppermute | solution.py:151
  178.6 34.2 %collective-permute-start.12 = (bf16[3,128,1024]{2,1,0:T(8,128)(2,1)}, bf16[3,128,1024]{2,1,0:T(8,128)(2,1)}, u32[]{:S(2)}, u32[]{:S(2)}) collective-permute-start(bf16[3,128,1024]{2,1,0:T(8,128)(2,1)} %gather_fusion.8), channel_id=1, source_target_pairs={{0,16},{8,24},{16,0},{24,8},{1,17},{9,25},{17,1},{25,9},{2,18},{10... | collective-permute-start | bytes 2359304 | tf_op jit(solution)/shard_map/ppermute | solution.py:151
  182.0 31.5 %collective-permute-start.13 = (bf16[3,128,1024]{2,1,0:T(8,128)(2,1)}, bf16[3,128,1024]{2,1,0:T(8,128)(2,1)}, u32[]{:S(2)}, u32[]{:S(2)}) collective-permute-start(bf16[3,128,1024]{2,1,0:T(8,128)(2,1)} %gather_fusion.9), channel_id=1, source_target_pairs={{0,24},{8,0},{16,8},{24,16},{1,25},{9,1},{17,9},{25,17},{2,26},{10... | collective-permute-start | bytes 2359304 | tf_op jit(solution)/shard_map/ppermute | solution.py:151
  185.0 28.7 %copy-start.5 = (bf16[3,128,1024]{2,1,0:T(8,128)(2,1)S(1)}, bf16[3,128,1024]{2,1,0:T(8,128)(2,1)}, u32[]{:S(2)}) copy-start(bf16[3,128,1024]{2,1,0:T(8,128)(2,1)} %gather_fusion.6) | copy-start | bytes 2359300
  240.1 37.9 %all-to-all-start.3 = ((bf16[8,128,256]{2,1,0:T(8,128)(2,1)}), bf16[8,128,256]{2,1,0:T(8,128)(2,1)S(1)}, u32[]{:S(2)}, u32[]{:S(2)}) async-start(bf16[8,128,256]{2,1,0:T(8,128)(2,1)} %broadcast_in_dim.61), calls=%async_computation.3 | async-start | bytes 1048576 | tf_op jit(solution)/shard_map/all_to_all | solution.py:223
  245.9 32.0 %collective-permute-start.3 = (bf16[512,1024]{1,0:T(8,128)(2,1)}, bf16[512,1024]{1,0:T(8,128)(2,1)S(1)}, u32[]{:S(2)}, u32[]{:S(2)}) collective-permute-start(bf16[512,1024]{1,0:T(8,128)(2,1)} %slice.42), channel_id=1, source_target_pairs={{0,2},{2,4},{4,6},{6,7},{7,5},{5,3},{3,1},{1,0},{8,10},{10,12},{12... | collective-permute-start | bytes 3145736 | tf_op jit(solution)/shard_map/ppermute | solution.py:189
  250.2 27.7 %collective-permute-start.7 = (bf16[512,1024]{1,0:T(8,128)(2,1)}, bf16[512,1024]{1,0:T(8,128)(2,1)S(1)}, u32[]{:S(2)}, u32[]{:S(2)}) collective-permute-start(bf16[512,1024]{1,0:T(8,128)(2,1)} %slice.43), channel_id=1, source_target_pairs={{2,0},{4,2},{6,4},{7,6},{5,7},{3,5},{1,3},{0,1},{10,8},{12,10},{14... | collective-permute-start | bytes 3145736 | tf_op jit(solution)/shard_map/ppermute | solution.py:190
  277.9 1.2 copy-start.7
  277.9 1.5 copy-start.8
  279.4 21.9 %copy-start.1 = (s32[8]{0:T(128)S(1)}, s32[8]{0:T(128)}, u32[]{:S(2)}) copy-start(s32[8]{0:T(128)} %param.13) | copy-start | bytes 100
  (3 other events, 2.6 us)
